TPU v7x, 32 devices: a whole 2x2x4 slice. The times are simulated.
32 devices in a mesh: groups: 2 (over y), frames: 4 (over z), rows: 4 (over x, core).
Axes of the slice: x: 2, y: 2, z: 4, core: 2. Of those that a mesh axis runs over, the one named last changes fastest.
Arguments:
- latents: bfloat16 [16, 8, 16, 1280], P('rows', ('groups', 'frames')), parts along dimension 1, may hold values from -6 to 6
- spatial_weight: bfloat16 [3, 3, 1280, 1280], P(None, None, None, 'rows'), may hold values from -0.0546875 to 0.0546875
- spatial_bias: float32 [1280], P('rows'), may hold values from -3 to 3
- norm_gain: float32 [1280], P('rows'), may hold values from 0.1 to 1.9
- norm_shift: float32 [1280], P('rows'), may hold values from -3 to 3
- temporal_weight: bfloat16 [3, 1280, 1280], P(None, 'rows'), may hold values from -0.09375 to 0.09375
- temporal_bias: float32 [1280], replicated, may hold values from -3 to 3
- token_gain: float32 [1280], replicated, may hold values from 0.1 to 1.9
- query_weight: bfloat16 [1280, 1024], P(None, 'rows'), may hold values from -4 to 4
- key_weight: bfloat16 [1280, 1024], P(None, 'rows'), may hold values from -4 to 4
- value_weight: bfloat16 [1280, 1024], P(None, 'rows'), may hold values from -0.15625 to 0.15625
- output_weight: bfloat16 [1024, 1280], P('rows'), may hold values from -0.1875 to 0.1875
Outputs:
- denoised: bfloat16 [16, 8, 16, 1280], P('rows', ('groups', 'frames')), parts along dimension 1
There are 2 independent parts, one for each index of `groups`. A program takes and returns all parts, laid end to end along the dimension named above; an argument that names none is the same for every part. Nothing has to cross between parts.
All inputs are finite; a program needn't handle non-finite values.
Results may differ from a plain program's by a relative error of at most 0.034.
Values may be sent and summed in bfloat16 or wider, within the bound.
A program may use at most 128 MiB of HBM per device.

v0:
```python
import math

import jax
import jax.numpy as jnp
from jax import lax
from jax.sharding import PartitionSpec as P

HD = 64
NORM_GROUPS = 32


def padded_2(array, sides, width):
    for axis, dim in sides:
        peers, length = (lax.axis_size(axis), array.shape[dim])
        up = [(i, (i + 1) % peers) for i in range(peers - 1)]
        down = [(j, i) for i, j in up]
        last = lax.slice_in_dim(array, length - width, length, axis=dim)
        leading = lax.slice_in_dim(array, 0, width, axis=dim)
        before = lax.ppermute(last, axis, up)
        after = lax.ppermute(leading, axis, down)
        array = jnp.concatenate([before, array, after], axis=dim)
    return array


def shifted_2(value, axis, steps):
    count = lax.axis_size(axis)
    pairs = [(source, (source + steps) % count) for source in range(count)]
    return lax.ppermute(value, axis, pairs)


def conv_plane(field, weight, bias):
    rows_n, frames_n, cols_n, chans = field.shape
    padded = jnp.pad(field, ((1, 1), (0, 0), (1, 1), (0, 0)))
    total = jnp.zeros((rows_n * frames_n * cols_n, weight.shape[3]), jnp.float32)
    for row_off in range(3):
        for col_off in range(3):
            window = padded[row_off : row_off + rows_n, :, col_off : col_off + cols_n, :].reshape(
                -1, chans
            )
            total = total + jnp.dot(
                window, weight[row_off, col_off], preferred_element_type=jnp.float32
            )
    return total.reshape(rows_n, frames_n, cols_n, -1) + bias


def layer_norm(field, token_gain):
    flat = field.astype(jnp.float32)
    token_mean = jnp.mean(flat, axis=-1, keepdims=True)
    shifted = flat - token_mean
    token_var = jnp.mean(shifted * shifted, axis=-1, keepdims=True)
    return (shifted / jnp.sqrt(token_var + 1e-05) * token_gain).astype(jnp.bfloat16)


def attend(queries, carried, keys, values):
    block = queries.shape[0]
    head_count = queries.shape[1]
    block_count = keys.shape[0] // block
    key_blocks = keys.reshape(block_count, block, head_count, HD)
    value_blocks = values.reshape(block_count, block, head_count, HD)
    scale = 1.0 / math.sqrt(HD)

    def visit_block(state, block_pair):
        running_max, denominator, numerator = state
        key_block, value_block = block_pair
        scores = (
            jnp.einsum("qhd,khd->qhk", queries, key_block, preferred_element_type=jnp.float32)
            * scale
        )
        new_max = jnp.maximum(running_max, jnp.max(scores, axis=-1))
        shrink = jnp.exp(running_max - new_max)
        weights = jnp.exp(scores - new_max[..., None])
        denominator = denominator * shrink + jnp.sum(weights, axis=-1)
        numerator = numerator * shrink[..., None] + jnp.einsum(
            "qhk,khd->qhd",
            weights.astype(jnp.bfloat16),
            value_block,
            preferred_element_type=jnp.float32,
        )
        return ((new_max, denominator, numerator), None)

    result, _ = lax.scan(visit_block, carried, (key_blocks, value_blocks))
    return result


def body(
    latents,
    spatial_weight,
    spatial_bias,
    norm_gain,
    norm_shift,
    temporal_weight,
    temporal_bias,
    token_gain,
    query_weight,
    key_weight,
    value_weight,
    output_weight,
):
    row_count, frame_count, width_cells, channels = latents.shape
    plane = lax.all_gather(latents, "rows", axis=0, tiled=True)
    plane_rows = plane.shape[0]
    local_out = spatial_weight.shape[3]
    spatial = conv_plane(plane, spatial_weight, spatial_bias)
    local_groups = NORM_GROUPS // lax.axis_size("rows")
    grouped = spatial.reshape(plane_rows, frame_count, width_cells, local_groups, -1)
    group_mean = jnp.mean(grouped, axis=(0, 2, 4), keepdims=True)
    centred = grouped - group_mean
    group_var = jnp.mean(centred * centred, axis=(0, 2, 4), keepdims=True)
    scaled = (centred / jnp.sqrt(group_var + 1e-05)).reshape(
        plane_rows, frame_count, width_cells, local_out
    ) * norm_gain + norm_shift
    activated = jax.nn.silu(scaled).astype(jnp.bfloat16)
    rim = padded_2(activated, (("frames", 1),), 1)
    row_total = row_count * lax.axis_size("rows")
    row_piece = rim
    total = jnp.zeros((row_total * frame_count * width_cells, channels), jnp.float32)
    for lag_index in range(3):
        window = row_piece[:, lag_index : lag_index + frame_count].reshape(-1, local_out)
        total = total + jnp.dot(
            window, temporal_weight[lag_index], preferred_element_type=jnp.float32
        )
    temporal = lax.psum_scatter(
        total.reshape(row_total, frame_count, width_cells, channels).astype(jnp.bfloat16),
        "rows",
        scatter_dimension=0,
        tiled=True,
    ).astype(jnp.float32)
    hidden = (latents.astype(jnp.float32) + temporal + temporal_bias).astype(jnp.bfloat16)
    normed_all = lax.all_gather(layer_norm(hidden, token_gain), "rows", axis=0, tiled=True)
    flat = normed_all.reshape(-1, channels)
    head_cols = query_weight.shape[1]
    head_count = head_cols // HD
    token_count = flat.shape[0]
    queries = jnp.dot(flat, query_weight, preferred_element_type=jnp.float32).astype(jnp.bfloat16)
    keys = jnp.dot(flat, key_weight, preferred_element_type=jnp.float32).astype(jnp.bfloat16)
    values = jnp.dot(flat, value_weight, preferred_element_type=jnp.float32).astype(jnp.bfloat16)
    start_state = (
        jnp.full((token_count, head_count), -1e30, jnp.float32),
        jnp.zeros((token_count, head_count), jnp.float32),
        jnp.zeros((token_count, head_count, HD), jnp.float32),
    )
    local_keys = keys.reshape(token_count, head_count, HD)
    local_values = values.reshape(token_count, head_count, HD)

    def travel(turn, state):
        query_moving, running_max, denominator, numerator = state
        running_max, denominator, numerator = attend(
            query_moving, (running_max, denominator, numerator), local_keys, local_values
        )
        return (
            shifted_2(query_moving, "frames", 1),
            shifted_2(running_max.astype(jnp.bfloat16), "frames", 1).astype(running_max.dtype),
            shifted_2(denominator.astype(jnp.bfloat16), "frames", 1).astype(denominator.dtype),
            shifted_2(numerator.astype(jnp.bfloat16), "frames", 1).astype(numerator.dtype),
        )

    start_moving = queries.reshape(token_count, head_count, HD)
    final = lax.fori_loop(0, lax.axis_size("frames"), travel, (start_moving,) + start_state)
    denominator, numerator = (final[2], final[3])
    attended = (
        (numerator / denominator[..., None])
        .astype(jnp.bfloat16)
        .reshape(plane_rows, frame_count, width_cells, head_cols)
    )
    row_piece = attended
    mixed = lax.psum_scatter(
        jnp.dot(row_piece.reshape(-1, head_cols), output_weight, preferred_element_type=jnp.float32)
        .reshape(row_count * lax.axis_size("rows"), frame_count, width_cells, channels)
        .astype(jnp.bfloat16),
        "rows",
        scatter_dimension=0,
        tiled=True,
    ).astype(jnp.float32)
    return (hidden.astype(jnp.float32) + mixed).astype(jnp.bfloat16)


def solution(mesh):
    in_specs = (
        P("rows", ("groups", "frames"), None, None),
        P(None, None, None, "rows"),
        P("rows"),
        P("rows"),
        P("rows"),
        P(None, "rows", None),
        P(),
        P(),
        P(None, "rows"),
        P(None, "rows"),
        P(None, "rows"),
        P("rows", None),
    )
    out_specs = P("rows", ("groups", "frames"), None, None)
    return jax.shard_map(body, mesh=mesh, in_specs=in_specs, out_specs=out_specs, check_vma=False)
```

profile of v0, /device:TPU:0, one launch (start us, length us, event | category | flops | bytes accessed | tf_op | source)
XLA Modules:
  0.0 143.5 jit_solution(10929822833257368733)
XLA Ops:
  6.5 9.7 %all_gather.6 = bf16[16,1,16,1280]{3,2,1,0:T(8,128)(2,1)S(1)} all-gather(bf16[4,1,16,1280]{3,2,1,0:T(8,128)(2,1)} %param.14), channel_id=1, replica_groups=mesh['groups'=2,'frames'=4,'rows'=4] {'rows'}, dimensions={0}, use_global_device_ids=true | all-gather | bytes 819200 | tf_op jit(solution)/shard_map/all_gather | solution.py:100
  16.2 1.4 %pad_slice_fusion = (bf16[16,1,16,1280]{3,2,1,0:T(8,128)(2,1)S(1)}, bf16[16,1,16,1280]{3,2,1,0:T(8,128)(2,1)S(1)}, bf16[16,1,16,1280]{3,2,1,0:T(8,128)(2,1)S(1)}...) fusion(bf16[16,1,16,1280]{3,2,1,0:T(8,128)(2,1)S(1)} %all_gather.6), kind=kLoop, calls=%fused_computation.20 | loop fusion | bytes 5898240 | tf_op jit(solution)/shard_map/slice | solution.py:37
  17.7 2.2 %fusion.25 = f32[256,320]{0,1:T(8,128)S(1)} fusion(bf16[256,1280]{1,0:T(8,128)(2,1)S(1)} %bitcast.124, bf16[3,3,1280,320]{2,3,1,0:T(8,128)(2,1)} %param.15), kind=kOutput, calls=%fused_computation.52 | convolution fusion | flops 209715200 | bytes 1802240 | tf_op jit(solution)/shard_map/dot_general | solution.py:40
  22.8 0.5 add_reduce_fusion
  24.7 1.4 collective-permute-start.5
  26.1 4.6 %collective-permute-start.4 = (bf16[16,1,16,320]{3,2,0,1:T(8,128)(2,1)S(1)}, bf16[16,1,16,320]{3,2,0,1:T(8,128)(2,1)S(1)}, u32[]{:S(2)}, u32[]{:S(2)}) collective-permute-start(bf16[16,1,16,320]{3,2,0,1:T(8,128)(2,1)S(1)} %multiply_convert_fusion), channel_id=1, source_target_pairs={{0,4},{4,8},{8,12},{1,5},{5,9},{9,13},{2,6},{6,10},{10,14},{3,7},{... | collective-permute-start | bytes 491528 | tf_op jit(solution)/shard_map/ppermute | solution.py:19
  30.7 1.9 %fusion.14 = f32[256,1280]{1,0:T(8,128)S(1)} fusion(bf16[3,320,1280]{2,1,0:T(8,128)(2,1)} %param.19, f32[256,320]{0,1:T(8,128)S(1)} %get-tuple-element.149, f32[320]{0:T(512)S(1)} %copy-done.9, f32[320]{0:T(512)S(1)} %copy-done.10, f32[320]{0:T(512)S(1)} %div.73, f32[320]{0:T(512)S(1)} %sub.56, f32[320]{0:T(512)S(1)} %copy-done.7), kind=kOutput, calls=%fused_computation.41 | convolution fusion | flops 210534400 | bytes 2464000 | tf_op jit(solution)/shard_map/dot_general | solution.py:119
  32.7 1.2 collective-permute-done.5
  34.4 0.7 collective-permute-done.4
  35.1 1.4 fusion.10
  36.6 24.3 %reduce-scatter.3.cloned.1.call-done = bf16[4,1,16,1280]{3,2,0,1:T(8,128)(2,1)} async-done(((bf16[16,1,16,1280]{3,2,0,1:T(8,128)(2,1)}), bf16[4,1,16,1280]{3,2,0,1:T(8,128)(2,1)}) %reduce-scatter.3.cloned.1.call-update) | async-done | bytes 163856 | tf_op jit(solution)/shard_map/reduce_scatter | solution.py:122
  60.8 1.0 convert_reduce_fusion
  62.3 7.3 %all_gather.7 = bf16[16,1,16,1280]{3,2,1,0:T(8,128)(2,1)S(1)} all-gather(bf16[4,1,16,1280]{3,2,1,0:T(8,128)(2,1)S(1)} %fusion.47), channel_id=1, replica_groups=mesh['groups'=2,'frames'=4,'rows'=4] {'rows'}, dimensions={0}, use_global_device_ids=true | all-gather | bytes 819200 | tf_op jit(solution)/shard_map/all_gather | solution.py:129
  70.5 1.5 %convolution_convert_fusion.3 = bf16[256,256]{0,1:T(8,128)(2,1)S(1)} fusion(bf16[256,1280]{1,0:T(8,128)(2,1)S(1)} %bitcast.110, bf16[1280,256]{1,0:T(8,128)(2,1)} %param.22), kind=kOutput, calls=%fused_computation.38 | convolution fusion | flops 167837696 | bytes 1441792 | tf_op jit(solution)/shard_map/dot_general | solution.py:134
  72.0 40.9 %while.16 = (s32[]{:T(128)}, bf16[256,4,64]{0,2,1:T(8,128)(2,1)S(1)}, f32[256,4]{0,1:T(4,128)S(1)}, f32[256,4]{0,1:T(4,128)S(1)}, f32[256,4,64]{0,2,1:T(8,128)S(...) while((s32[]{:T(128)}, ...), condition=%wide.region_10.11_spmd.clone, body=%wide.region_7.10_spmd.clone.sunk | while | flops 69018624 | bytes 5722377 | solution.py:158
  72.9 1.5 %collective-permute-start.3 = (bf16[256,4,64]{0,2,1:T(8,128)(2,1)S(1)}, bf16[256,4,64]{0,2,1:T(8,128)(2,1)S(1)}, u32[]{:S(2)}, u32[]{:S(2)}) collective-permute-start(bf16[256,4,64]{0,2,1:T(8,128)(2,1)S(1)} %fusion.95), channel_id=1, source_target_pairs={{0,4},{4,8},{8,12},{12,0},{1,5},{5,9},{9,13},{13,1},{2,6},{6,10},{... | collective-permute-start | bytes 393224 | tf_op jit(solution)/shard_map/while/body/eval_jaxpr/ppermute | solution.py:28
  74.4 1.5 %collective-permute-start = (bf16[256,4,64]{0,2,1:T(8,128)(2,1)S(1)}, bf16[256,4,64]{0,2,1:T(8,128)(2,1)S(1)}, u32[]{:S(2)}, u32[]{:S(2)}) collective-permute-start(bf16[256,4,64]{0,2,1:T(8,128)(2,1)S(1)} %copy.49), channel_id=1, source_target_pairs={{0,4},{4,8},{8,12},{12,0},{1,5},{5,9},{9,13},{13,1},{2,6},{6,10},{... | collective-permute-start | bytes 393224 | tf_op jit(solution)/shard_map/while/body/eval_jaxpr/ppermute | solution.py:28
  75.9 1.5 %collective-permute-start.2 = (bf16[256,4]{0,1:T(4,128)(2,1)S(1)}, bf16[256,4]{0,1:T(4,128)(2,1)S(1)}, u32[]{:S(2)}, u32[]{:S(2)}) collective-permute-start(bf16[256,4]{0,1:T(4,128)(2,1)S(1)} %get-tuple-element.203), channel_id=1, source_target_pairs={{0,4},{4,8},{8,12},{12,0},{1,5},{5,9},{9,13},{13,1},{2,6},{6,10},{... | collective-permute-start | bytes 6152 | tf_op jit(solution)/shard_map/while/body/eval_jaxpr/ppermute | solution.py:28
  77.9 5.5 %collective-permute-done.2 = bf16[256,4]{0,1:T(4,128)(2,1)S(1)} collective-permute-done((bf16[256,4]{0,1:T(4,128)(2,1)S(1)}, bf16[256,4]{0,1:T(4,128)(2,1)S(1)}, u32[]{:S(2)}, u32[]{:S(2)}) %collective-permute-start.2) | collective-permute-done | bytes 2080 | tf_op jit(solution)/shard_map/while/body/eval_jaxpr/ppermute | solution.py:28
  84.4 1.2 collective-permute-start
  85.5 1.5 %collective-permute-start.2 = (bf16[256,4]{0,1:T(4,128)(2,1)S(1)}, bf16[256,4]{0,1:T(4,128)(2,1)S(1)}, u32[]{:S(2)}, u32[]{:S(2)}) collective-permute-start(bf16[256,4]{0,1:T(4,128)(2,1)S(1)} %get-tuple-element.203), channel_id=1, source_target_pairs={{0,4},{4,8},{8,12},{12,0},{1,5},{5,9},{9,13},{13,1},{2,6},{6,10},{... | collective-permute-start | bytes 6152 | tf_op jit(solution)/shard_map/while/body/eval_jaxpr/ppermute | solution.py:28
  87.0 2.3 %collective-permute-start.1 = (bf16[256,4]{0,1:T(4,128)(2,1)S(1)}, bf16[256,4]{0,1:T(4,128)(2,1)S(1)}, u32[]{:S(2)}, u32[]{:S(2)}) collective-permute-start(bf16[256,4]{0,1:T(4,128)(2,1)S(1)} %get-tuple-element.200), channel_id=1, source_target_pairs={{0,4},{4,8},{8,12},{12,0},{1,5},{5,9},{9,13},{13,1},{2,6},{6,10},{... | collective-permute-start | bytes 6152 | tf_op jit(solution)/shard_map/while/body/eval_jaxpr/ppermute | solution.py:28
  89.3 4.6 %collective-permute-done.2 = bf16[256,4]{0,1:T(4,128)(2,1)S(1)} collective-permute-done((bf16[256,4]{0,1:T(4,128)(2,1)S(1)}, bf16[256,4]{0,1:T(4,128)(2,1)S(1)}, u32[]{:S(2)}, u32[]{:S(2)}) %collective-permute-start.2) | collective-permute-done | bytes 2080 | tf_op jit(solution)/shard_map/while/body/eval_jaxpr/ppermute | solution.py:28
  95.0 0.8 collective-permute-start.2
  95.8 4.0 %collective-permute-start.1 = (bf16[256,4]{0,1:T(4,128)(2,1)S(1)}, bf16[256,4]{0,1:T(4,128)(2,1)S(1)}, u32[]{:S(2)}, u32[]{:S(2)}) collective-permute-start(bf16[256,4]{0,1:T(4,128)(2,1)S(1)} %get-tuple-element.200), channel_id=1, source_target_pairs={{0,4},{4,8},{8,12},{12,0},{1,5},{5,9},{9,13},{13,1},{2,6},{6,10},{... | collective-permute-start | bytes 6152 | tf_op jit(solution)/shard_map/while/body/eval_jaxpr/ppermute | solution.py:28
  99.9 3.7 %collective-permute-done.2 = bf16[256,4]{0,1:T(4,128)(2,1)S(1)} collective-permute-done((bf16[256,4]{0,1:T(4,128)(2,1)S(1)}, bf16[256,4]{0,1:T(4,128)(2,1)S(1)}, u32[]{:S(2)}, u32[]{:S(2)}) %collective-permute-start.2) | collective-permute-done | bytes 2080 | tf_op jit(solution)/shard_map/while/body/eval_jaxpr/ppermute | solution.py:28
  104.7 1.2 collective-permute-start.2
  105.9 3.7 %collective-permute-start.1 = (bf16[256,4]{0,1:T(4,128)(2,1)S(1)}, bf16[256,4]{0,1:T(4,128)(2,1)S(1)}, u32[]{:S(2)}, u32[]{:S(2)}) collective-permute-start(bf16[256,4]{0,1:T(4,128)(2,1)S(1)} %get-tuple-element.200), channel_id=1, source_target_pairs={{0,4},{4,8},{8,12},{12,0},{1,5},{5,9},{9,13},{13,1},{2,6},{6,10},{... | collective-permute-start | bytes 6152 | tf_op jit(solution)/shard_map/while/body/eval_jaxpr/ppermute | solution.py:28
  109.6 3.2 %collective-permute-done.2 = bf16[256,4]{0,1:T(4,128)(2,1)S(1)} collective-permute-done((bf16[256,4]{0,1:T(4,128)(2,1)S(1)}, bf16[256,4]{0,1:T(4,128)(2,1)S(1)}, u32[]{:S(2)}, u32[]{:S(2)}) %collective-permute-start.2) | collective-permute-done | bytes 2080 | tf_op jit(solution)/shard_map/while/body/eval_jaxpr/ppermute | solution.py:28
  113.3 1.2 fusion.11
  114.6 20.4 %reduce-scatter.5.cloned.1.call-done = bf16[4,1,16,1280]{3,2,0,1:T(8,128)(2,1)} async-done(((bf16[16,1,16,1280]{3,2,0,1:T(8,128)(2,1)}), bf16[4,1,16,1280]{3,2,0,1:T(8,128)(2,1)}) %reduce-scatter.5.cloned.1.call-update) | async-done | bytes 163856 | tf_op jit(solution)/shard_map/reduce_scatter | solution.py:166
  135.0 1.6 %fusion.46 = bf16[4,1,16,1280]{3,2,1,0:T(8,128)(2,1)} fusion(bf16[4,1,16,1280]{3,2,0,1:T(8,128)(2,1)} %reduce-scatter.5.cloned.1.call-done, bf16[4,1,16,1280]{3,2,0,1:T(8,128)(2,1)S(1)} %get-tuple-element.137), kind=kLoop, calls=%fused_computation.82 | loop fusion | flops 327680 | bytes 491520 | tf_op jit(solution)/shard_map/convert_element_type | solution.py:174
  (115 shorter events, 10.8 us)
Async XLA Ops:
  6.5 106.8 %copy-start = (bf16[256,1280]{1,0:T(8,128)(2,1)S(1)}, bf16[256,1280]{1,0:T(8,128)(2,1)}, u32[]{:S(2)}) copy-start(bf16[256,1280]{1,0:T(8,128)(2,1)} %param.25) | copy-start | bytes 1966084
  6.5 54.3 %reduce-scatter.3.cloned.1.call-start = ((), (), s32[]{:S(2)}) async-start(), calls=%async_computation.2 | async-start | bytes 819200 | tf_op jit(solution)/shard_map/reduce_scatter | solution.py:122
  16.2 3.6 %copy-start.1 = (bf16[3,3,1280,320]{2,3,1,0:T(8,128)(2,1)S(1)}, bf16[3,3,1280,320]{2,3,1,0:T(8,128)(2,1)}, u32[]{:S(2)}) copy-start(bf16[3,3,1280,320]{2,3,1,0:T(8,128)(2,1)} %param.15) | copy-start | bytes 22118404
  21.9 0.9 copy-start.7
  22.4 2.2 %copy-start.9 = (f32[320]{0:T(512)S(1)}, f32[320]{0:T(512)}, u32[]{:S(2)}) copy-start(f32[320]{0:T(512)} %param.18) | copy-start | bytes 3844
  22.4 2.2 %copy-start.10 = (f32[320]{0:T(512)S(1)}, f32[320]{0:T(512)}, u32[]{:S(2)}) copy-start(f32[320]{0:T(512)} %param.17) | copy-start | bytes 3844
  24.5 9.4 %copy-start.2 = (bf16[3,320,1280]{2,1,0:T(8,128)(2,1)S(1)}, bf16[3,320,1280]{2,1,0:T(8,128)(2,1)}, u32[]{:S(2)}) copy-start(bf16[3,320,1280]{2,1,0:T(8,128)(2,1)} %param.19) | copy-start | bytes 7372804
  24.7 9.2 %collective-permute-start.5 = (bf16[16,1,16,320]{3,2,0,1:T(8,128)(2,1)S(1)}, bf16[16,1,16,320]{3,2,0,1:T(8,128)(2,1)S(1)}, u32[]{:S(2)}, u32[]{:S(2)}) collective-permute-start(bf16[16,1,16,320]{3,2,0,1:T(8,128)(2,1)S(1)} %multiply_convert_fusion), channel_id=1, source_target_pairs={{4,0},{8,4},{12,8},{5,1},{9,5},{13,9},{6,2},{10,6},{14,10},{7,3},{... | collective-permute-start | bytes 491528 | tf_op jit(solution)/shard_map/ppermute | solution.py:20
  26.1 8.9 %collective-permute-start.4 = (bf16[16,1,16,320]{3,2,0,1:T(8,128)(2,1)S(1)}, bf16[16,1,16,320]{3,2,0,1:T(8,128)(2,1)S(1)}, u32[]{:S(2)}, u32[]{:S(2)}) collective-permute-start(bf16[16,1,16,320]{3,2,0,1:T(8,128)(2,1)S(1)} %multiply_convert_fusion), channel_id=1, source_target_pairs={{0,4},{4,8},{8,12},{1,5},{5,9},{9,13},{2,6},{6,10},{10,14},{3,7},{... | collective-permute-start | bytes 491528 | tf_op jit(solution)/shard_map/ppermute | solution.py:19
  35.1 25.7 %copy-start.5 = (bf16[4,1,16,1280]{3,2,1,0:T(8,128)(2,1)S(1)}, bf16[4,1,16,1280]{3,2,1,0:T(8,128)(2,1)}, u32[]{:S(2)}) copy-start(bf16[4,1,16,1280]{3,2,1,0:T(8,128)(2,1)} %param.14) | copy-start | bytes 491524
  35.1 25.8 %copy-start.6 = (f32[1280]{0:T(1024)S(1)}, f32[1280]{0:T(1024)}, u32[]{:S(2)}) copy-start(f32[1280]{0:T(1024)} %param.20) | copy-start | bytes 15364
  35.1 27.0 %copy-start.8 = (f32[1280]{0:T(1024)S(1)}, f32[1280]{0:T(1024)}, u32[]{:S(2)}) copy-start(f32[1280]{0:T(1024)} %param.21) | copy-start | bytes 15364
  35.1 34.5 %copy-start.3 = (bf16[1280,256]{1,0:T(8,128)(2,1)S(1)}, bf16[1280,256]{1,0:T(8,128)(2,1)}, u32[]{:S(2)}) copy-start(bf16[1280,256]{1,0:T(8,128)(2,1)} %param.23) | copy-start | bytes 1966084
  36.4 33.6 %copy-start.4 = (bf16[1280,256]{1,0:T(8,128)(2,1)S(1)}, bf16[1280,256]{1,0:T(8,128)(2,1)}, u32[]{:S(2)}) copy-start(bf16[1280,256]{1,0:T(8,128)(2,1)} %param.24) | copy-start | bytes 1966084
  36.5 98.5 %reduce-scatter.5.cloned.1.call-start = ((), (), s32[]{:S(2)}) async-start(), calls=%async_computation.3 | async-start | bytes 819200 | tf_op jit(solution)/shard_map/reduce_scatter | solution.py:166
  72.9 10.5 %collective-permute-start.3 = (bf16[256,4,64]{0,2,1:T(8,128)(2,1)S(1)}, bf16[256,4,64]{0,2,1:T(8,128)(2,1)S(1)}, u32[]{:S(2)}, u32[]{:S(2)}) collective-permute-start(bf16[256,4,64]{0,2,1:T(8,128)(2,1)S(1)} %fusion.95), channel_id=1, source_target_pairs={{0,4},{4,8},{8,12},{12,0},{1,5},{5,9},{9,13},{13,1},{2,6},{6,10},{... | collective-permute-start | bytes 393224 | tf_op jit(solution)/shard_map/while/body/eval_jaxpr/ppermute | solution.py:28
  74.4 9.0 %collective-permute-start = (bf16[256,4,64]{0,2,1:T(8,128)(2,1)S(1)}, bf16[256,4,64]{0,2,1:T(8,128)(2,1)S(1)}, u32[]{:S(2)}, u32[]{:S(2)}) collective-permute-start(bf16[256,4,64]{0,2,1:T(8,128)(2,1)S(1)} %copy.49), channel_id=1, source_target_pairs={{0,4},{4,8},{8,12},{12,0},{1,5},{5,9},{9,13},{13,1},{2,6},{6,10},{... | collective-permute-start | bytes 393224 | tf_op jit(solution)/shard_map/while/body/eval_jaxpr/ppermute | solution.py:28
  75.9 7.4 %collective-permute-start.2 = (bf16[256,4]{0,1:T(4,128)(2,1)S(1)}, bf16[256,4]{0,1:T(4,128)(2,1)S(1)}, u32[]{:S(2)}, u32[]{:S(2)}) collective-permute-start(bf16[256,4]{0,1:T(4,128)(2,1)S(1)} %get-tuple-element.203), channel_id=1, source_target_pairs={{0,4},{4,8},{8,12},{12,0},{1,5},{5,9},{9,13},{13,1},{2,6},{6,10},{... | collective-permute-start | bytes 6152 | tf_op jit(solution)/shard_map/while/body/eval_jaxpr/ppermute | solution.py:28
  77.4 6.0 %collective-permute-start.1 = (bf16[256,4]{0,1:T(4,128)(2,1)S(1)}, bf16[256,4]{0,1:T(4,128)(2,1)S(1)}, u32[]{:S(2)}, u32[]{:S(2)}) collective-permute-start(bf16[256,4]{0,1:T(4,128)(2,1)S(1)} %get-tuple-element.200), channel_id=1, source_target_pairs={{0,4},{4,8},{8,12},{12,0},{1,5},{5,9},{9,13},{13,1},{2,6},{6,10},{... | collective-permute-start | bytes 6152 | tf_op jit(solution)/shard_map/while/body/eval_jaxpr/ppermute | solution.py:28
  84.3 9.6 %collective-permute-start.3 = (bf16[256,4,64]{0,2,1:T(8,128)(2,1)S(1)}, bf16[256,4,64]{0,2,1:T(8,128)(2,1)S(1)}, u32[]{:S(2)}, u32[]{:S(2)}) collective-permute-start(bf16[256,4,64]{0,2,1:T(8,128)(2,1)S(1)} %fusion.95), channel_id=1, source_target_pairs={{0,4},{4,8},{8,12},{12,0},{1,5},{5,9},{9,13},{13,1},{2,6},{6,10},{... | collective-permute-start | bytes 393224 | tf_op jit(solution)/shard_map/while/body/eval_jaxpr/ppermute | solution.py:28
  84.4 9.6 %collective-permute-start = (bf16[256,4,64]{0,2,1:T(8,128)(2,1)S(1)}, bf16[256,4,64]{0,2,1:T(8,128)(2,1)S(1)}, u32[]{:S(2)}, u32[]{:S(2)}) collective-permute-start(bf16[256,4,64]{0,2,1:T(8,128)(2,1)S(1)} %copy.49), channel_id=1, source_target_pairs={{0,4},{4,8},{8,12},{12,0},{1,5},{5,9},{9,13},{13,1},{2,6},{6,10},{... | collective-permute-start | bytes 393224 | tf_op jit(solution)/shard_map/while/body/eval_jaxpr/ppermute | solution.py:28
  85.5 8.4 %collective-permute-start.2 = (bf16[256,4]{0,1:T(4,128)(2,1)S(1)}, bf16[256,4]{0,1:T(4,128)(2,1)S(1)}, u32[]{:S(2)}, u32[]{:S(2)}) collective-permute-start(bf16[256,4]{0,1:T(4,128)(2,1)S(1)} %get-tuple-element.203), channel_id=1, source_target_pairs={{0,4},{4,8},{8,12},{12,0},{1,5},{5,9},{9,13},{13,1},{2,6},{6,10},{... | collective-permute-start | bytes 6152 | tf_op jit(solution)/shard_map/while/body/eval_jaxpr/ppermute | solution.py:28
  87.0 6.9 %collective-permute-start.1 = (bf16[256,4]{0,1:T(4,128)(2,1)S(1)}, bf16[256,4]{0,1:T(4,128)(2,1)S(1)}, u32[]{:S(2)}, u32[]{:S(2)}) collective-permute-start(bf16[256,4]{0,1:T(4,128)(2,1)S(1)} %get-tuple-element.200), channel_id=1, source_target_pairs={{0,4},{4,8},{8,12},{12,0},{1,5},{5,9},{9,13},{13,1},{2,6},{6,10},{... | collective-permute-start | bytes 6152 | tf_op jit(solution)/shard_map/while/body/eval_jaxpr/ppermute | solution.py:28
  94.9 8.8 %collective-permute-start.3 = (bf16[256,4,64]{0,2,1:T(8,128)(2,1)S(1)}, bf16[256,4,64]{0,2,1:T(8,128)(2,1)S(1)}, u32[]{:S(2)}, u32[]{:S(2)}) collective-permute-start(bf16[256,4,64]{0,2,1:T(8,128)(2,1)S(1)} %fusion.95), channel_id=1, source_target_pairs={{0,4},{4,8},{8,12},{12,0},{1,5},{5,9},{9,13},{13,1},{2,6},{6,10},{... | collective-permute-start | bytes 393224 | tf_op jit(solution)/shard_map/while/body/eval_jaxpr/ppermute | solution.py:28
  94.9 8.7 %collective-permute-start = (bf16[256,4,64]{0,2,1:T(8,128)(2,1)S(1)}, bf16[256,4,64]{0,2,1:T(8,128)(2,1)S(1)}, u32[]{:S(2)}, u32[]{:S(2)}) collective-permute-start(bf16[256,4,64]{0,2,1:T(8,128)(2,1)S(1)} %copy.49), channel_id=1, source_target_pairs={{0,4},{4,8},{8,12},{12,0},{1,5},{5,9},{9,13},{13,1},{2,6},{6,10},{... | collective-permute-start | bytes 393224 | tf_op jit(solution)/shard_map/while/body/eval_jaxpr/ppermute | solution.py:28
  95.0 8.6 %collective-permute-start.2 = (bf16[256,4]{0,1:T(4,128)(2,1)S(1)}, bf16[256,4]{0,1:T(4,128)(2,1)S(1)}, u32[]{:S(2)}, u32[]{:S(2)}) collective-permute-start(bf16[256,4]{0,1:T(4,128)(2,1)S(1)} %get-tuple-element.203), channel_id=1, source_target_pairs={{0,4},{4,8},{8,12},{12,0},{1,5},{5,9},{9,13},{13,1},{2,6},{6,10},{... | collective-permute-start | bytes 6152 | tf_op jit(solution)/shard_map/while/body/eval_jaxpr/ppermute | solution.py:28
  95.8 7.8 %collective-permute-start.1 = (bf16[256,4]{0,1:T(4,128)(2,1)S(1)}, bf16[256,4]{0,1:T(4,128)(2,1)S(1)}, u32[]{:S(2)}, u32[]{:S(2)}) collective-permute-start(bf16[256,4]{0,1:T(4,128)(2,1)S(1)} %get-tuple-element.200), channel_id=1, source_target_pairs={{0,4},{4,8},{8,12},{12,0},{1,5},{5,9},{9,13},{13,1},{2,6},{6,10},{... | collective-permute-start | bytes 6152 | tf_op jit(solution)/shard_map/while/body/eval_jaxpr/ppermute | solution.py:28
  104.6 8.3 %collective-permute-start.3 = (bf16[256,4,64]{0,2,1:T(8,128)(2,1)S(1)}, bf16[256,4,64]{0,2,1:T(8,128)(2,1)S(1)}, u32[]{:S(2)}, u32[]{:S(2)}) collective-permute-start(bf16[256,4,64]{0,2,1:T(8,128)(2,1)S(1)} %fusion.95), channel_id=1, source_target_pairs={{0,4},{4,8},{8,12},{12,0},{1,5},{5,9},{9,13},{13,1},{2,6},{6,10},{... | collective-permute-start | bytes 393224 | tf_op jit(solution)/shard_map/while/body/eval_jaxpr/ppermute | solution.py:28
  104.6 8.2 %collective-permute-start = (bf16[256,4,64]{0,2,1:T(8,128)(2,1)S(1)}, bf16[256,4,64]{0,2,1:T(8,128)(2,1)S(1)}, u32[]{:S(2)}, u32[]{:S(2)}) collective-permute-start(bf16[256,4,64]{0,2,1:T(8,128)(2,1)S(1)} %copy.49), channel_id=1, source_target_pairs={{0,4},{4,8},{8,12},{12,0},{1,5},{5,9},{9,13},{13,1},{2,6},{6,10},{... | collective-permute-start | bytes 393224 | tf_op jit(solution)/shard_map/while/body/eval_jaxpr/ppermute | solution.py:28
  104.7 8.1 %collective-permute-start.2 = (bf16[256,4]{0,1:T(4,128)(2,1)S(1)}, bf16[256,4]{0,1:T(4,128)(2,1)S(1)}, u32[]{:S(2)}, u32[]{:S(2)}) collective-permute-start(bf16[256,4]{0,1:T(4,128)(2,1)S(1)} %get-tuple-element.203), channel_id=1, source_target_pairs={{0,4},{4,8},{8,12},{12,0},{1,5},{5,9},{9,13},{13,1},{2,6},{6,10},{... | collective-permute-start | bytes 6152 | tf_op jit(solution)/shard_map/while/body/eval_jaxpr/ppermute | solution.py:28
  105.9 7.0 %collective-permute-start.1 = (bf16[256,4]{0,1:T(4,128)(2,1)S(1)}, bf16[256,4]{0,1:T(4,128)(2,1)S(1)}, u32[]{:S(2)}, u32[]{:S(2)}) collective-permute-start(bf16[256,4]{0,1:T(4,128)(2,1)S(1)} %get-tuple-element.200), channel_id=1, source_target_pairs={{0,4},{4,8},{8,12},{12,0},{1,5},{5,9},{9,13},{13,1},{2,6},{6,10},{... | collective-permute-start | bytes 6152 | tf_op jit(solution)/shard_map/while/body/eval_jaxpr/ppermute | solution.py:28
Sparse Core Ops, SparseCore 0:
  36.6 24.1 reduce-scatter.2
  114.7 20.2 reduce-scatter.4
where the time goes:
time: 144 us; the launch traced here: 143 us
  waiting for transfers between devices  63.8 us (44%)
  starting transfers between devices  26 us (18%)
  blocking collectives  17 us (12%)
  matrix products  15.3 us (11%)
  between operations  13.7 us (10%)
  other arithmetic  4.55 us (3%)
  local copies, waits for them, and re-layouts  2.77 us (2%)
    reduce_scatter x1, waiting for transfers between devices, body(): lax.psum_scatter(total.reshape(row_total, frame_count, width_cells, chann...  24.3 us
    reduce_scatter x1, waiting for transfers between devices, body(): lax.psum_scatter(jnp.dot(row_piece.reshape(-1, head_cols), output_weight,...  20.4 us
    ppermute x16, starting transfers between devices, shifted_2(): return lax.ppermute(value, axis, pairs)  20 us
    ppermute x16, waiting for transfers between devices, shifted_2(): return lax.ppermute(value, axis, pairs)  17.2 us
    all_gather x1, blocking collectives, body(): plane = lax.all_gather(latents, 'rows', axis=0, tiled=True)  9.69 us
    all_gather x1, blocking collectives, body(): lax.all_gather(layer_norm(hidden, token_gain), 'rows', axis=0, tiled=True)  7.3 us
    dot_general x9, matrix products, conv_plane(): jnp.dot(window, weight[row_off, col_off], preferred_element_type=jnp.floa...  5.55 us
    ppermute x1, starting transfers between devices, padded_2(): before = lax.ppermute(last, axis, up)  4.56 us
  transfers between devices with their start and end apart: 20, of which 8 were waited for; matrix products, arithmetic and copies ran while one was open for 2% of the time, Pallas kernels for 0%

commit v1 on v0

--- a/solution.py
+++ b/solution.py
@@ -1,8 +1,11 @@
+import functools
 import math
 
 import jax
 import jax.numpy as jnp
 from jax import lax
+from jax.experimental import pallas as pl
+from jax.experimental.pallas import tpu as pltpu
 from jax.sharding import PartitionSpec as P
 
 HD = 64
@@ -174,6 +177,480 @@
     return (hidden.astype(jnp.float32) + mixed).astype(jnp.bfloat16)
 
 
+MESH = pl.DeviceIdType.MESH
+DMA = pltpu.SemaphoreType.DMA
+VMEM_SPEC = pl.BlockSpec(memory_space=pltpu.VMEM)
+ANY_SPEC = pl.BlockSpec(memory_space=pl.ANY)
+BF16 = jnp.bfloat16
+F32 = jnp.float32
+VMEM_LIMIT = 40 << 20
+PARTS = 2
+
+
+def remote(src, dst, send, recv, axis, peer):
+    return pltpu.make_async_remote_copy(
+        src_ref=src,
+        dst_ref=dst,
+        send_sem=send,
+        recv_sem=recv,
+        device_id={axis: peer},
+        device_id_type=MESH,
+    )
+
+
+def greet(barrier, axis, peer):
+    pl.semaphore_signal(barrier, inc=1, device_id={axis: peer}, device_id_type=MESH)
+
+
+class Gather:
+    def __init__(self, block, out, send, recv):
+        me = lax.axis_index("rows")
+        near, far = me ^ 1, me ^ 2
+        step = block.shape[0] // PARTS
+        self.far, self.onward = [], []
+        for part in range(PARTS):
+            piece = pl.ds(part * step, step)
+            self.far.append(
+                remote(
+                    block.at[piece],
+                    out.at[me, piece],
+                    send.at[part],
+                    recv.at[part],
+                    "rows",
+                    far,
+                )
+            )
+            self.onward.append(
+                remote(
+                    out.at[far, piece],
+                    out.at[far, piece],
+                    send.at[PARTS + part],
+                    recv.at[PARTS + part],
+                    "rows",
+                    near,
+                )
+            )
+        self.near = remote(
+            block, out.at[me], send.at[2 * PARTS], recv.at[2 * PARTS], "rows", near
+        )
+
+    def start(self):
+        for copy in self.far:
+            copy.start()
+        self.near.start()
+
+    def finish(self):
+        for copy, onward in zip(self.far, self.onward):
+            copy.wait_recv()
+            onward.start()
+        for copy in self.far:
+            copy.wait_send()
+        self.near.wait()
+        for onward in self.onward:
+            onward.wait()
+
+
+def reduce_rows(term, sent, got_near, got_far, send, recv):
+    me = lax.axis_index("rows")
+    near, far = me ^ 1, me ^ 2
+    copies = []
+    for slot, block in enumerate((far ^ 1, near)):
+        sent[slot] = term(block).astype(BF16)
+        copy = remote(
+            sent.at[slot], got_near.at[slot], send.at[slot], recv.at[slot], "rows", near
+        )
+        copy.start()
+        copies.append(copy)
+    mine = term(far)
+    copies[0].wait_recv()
+    sent[2] = (mine + got_near[0].astype(F32)).astype(BF16)
+    across = remote(sent.at[2], got_far, send.at[2], recv.at[2], "rows", far)
+    across.start()
+    mine = term(me)
+    copies[1].wait_recv()
+    mine = mine + got_near[1].astype(F32)
+    across.wait_recv()
+    total = mine + got_far[...].astype(F32)
+    for copy in copies + [across]:
+        copy.wait_send()
+    return total
+
+
+def gather_kernel(x_ref, out_ref, send, recv):
+    me = lax.axis_index("rows")
+    barrier = pltpu.get_barrier_semaphore()
+    greet(barrier, "rows", me ^ 1)
+    greet(barrier, "rows", me ^ 2)
+    pl.semaphore_wait(barrier, 2)
+    gather = Gather(x_ref, out_ref, send, recv)
+    gather.start()
+    out_ref[me] = x_ref[...]
+    gather.finish()
+
+
+def temporal_kernel(
+    frames,
+    act,
+    weight_hbm,
+    latents,
+    bias,
+    gain,
+    hidden_ref,
+    normed_all,
+    weight,
+    halo,
+    sent,
+    got_near,
+    got_far,
+    normed,
+    load_sem,
+    halo_send,
+    halo_recv,
+    sum_send,
+    sum_recv,
+    gat_send,
+    gat_recv,
+):
+    load = pltpu.make_async_copy(weight_hbm, weight, load_sem)
+    load.start()
+    me = lax.axis_index("rows")
+    frame = lax.axis_index("frames")
+    has_prev, has_next = frame > 0, frame < frames - 1
+    prev = jnp.maximum(frame - 1, 0)
+    later = jnp.minimum(frame + 1, frames - 1)
+    barrier = pltpu.get_barrier_semaphore()
+    greet(barrier, "rows", me ^ 1)
+    greet(barrier, "rows", me ^ 2)
+
+    @pl.when(has_prev)
+    def _():
+        greet(barrier, "frames", prev)
+
+    @pl.when(has_next)
+    def _():
+        greet(barrier, "frames", later)
+
+    pl.semaphore_wait(barrier, 2 + has_prev.astype(jnp.int32) + has_next.astype(jnp.int32))
+
+    up = remote(act, halo.at[0], halo_send.at[0], halo_recv.at[0], "frames", later)
+    down = remote(act, halo.at[1], halo_send.at[1], halo_recv.at[1], "frames", prev)
+
+    @pl.when(has_next)
+    def _():
+        up.start()
+
+    @pl.when(has_prev)
+    def _():
+        down.start()
+
+    load.wait()
+
+    @pl.when(has_prev)
+    def _():
+        up.wait_recv()
+
+    @pl.when(jnp.logical_not(has_prev))
+    def _():
+        halo[0] = jnp.zeros(halo.shape[1:], halo.dtype)
+
+    @pl.when(has_next)
+    def _():
+        down.wait_recv()
+
+    @pl.when(jnp.logical_not(has_next))
+    def _():
+        halo[1] = jnp.zeros(halo.shape[1:], halo.dtype)
+
+    size = latents.shape[0]
+
+    def term(block):
+        rows = pl.ds(pl.multiple_of(block * size, size), size)
+        total = jnp.dot(act[rows, :], weight[1], preferred_element_type=F32)
+        total += jnp.dot(halo[0, rows, :], weight[0], preferred_element_type=F32)
+        total += jnp.dot(halo[1, rows, :], weight[2], preferred_element_type=F32)
+        return total
+
+    temporal = reduce_rows(term, sent, got_near, got_far, sum_send, sum_recv)
+    hidden = (latents[...].astype(F32) + temporal + bias[...]).astype(BF16)
+    hidden_ref[...] = hidden
+    flat = hidden.astype(F32)
+    shifted = flat - jnp.mean(flat, axis=-1, keepdims=True)
+    var = jnp.mean(shifted * shifted, axis=-1, keepdims=True)
+    value = (shifted / jnp.sqrt(var + 1e-05) * gain[...]).astype(BF16)
+    normed[...] = value
+    gather = Gather(normed, normed_all, gat_send, gat_recv)
+    gather.start()
+    normed_all[me] = value
+    gather.finish()
+
+    @pl.when(has_next)
+    def _():
+        up.wait_send()
+
+    @pl.when(has_prev)
+    def _():
+        down.wait_send()
+
+
+def attention_kernel(
+    frames,
+    q_ref,
+    k_ref,
+    v_ref,
+    weight_hbm,
+    hidden,
+    out_ref,
+    weight,
+    got,
+    keys,
+    values,
+    done,
+    back,
+    att,
+    sent,
+    got_near,
+    got_far,
+    load_sem,
+    in_send,
+    in_recv,
+    out_send,
+    out_recv,
+    sum_send,
+    sum_recv,
+):
+    load = pltpu.make_async_copy(weight_hbm, weight, load_sem)
+    load.start()
+    me = lax.axis_index("rows")
+    frame = lax.axis_index("frames")
+    barrier = pltpu.get_barrier_semaphore()
+    greet(barrier, "rows", me ^ 1)
+    greet(barrier, "rows", me ^ 2)
+    for turn in range(1, frames):
+        greet(barrier, "frames", lax.rem(frame + turn, frames))
+    pl.semaphore_wait(barrier, frames + 1)
+    copies = []
+    for kind, ref in ((0, k_ref), (1, q_ref), (2, v_ref)):
+        for turn in range(1, frames):
+            peer = lax.rem(frame + turn, frames)
+            copy = remote(
+                ref.at[peer],
+                got.at[kind, frame],
+                in_send.at[kind, turn],
+                in_recv.at[kind, turn],
+                "frames",
+                peer,
+            )
+            copy.start()
+            copies.append(copy)
+        got[kind, frame] = ref[frame]
+    for copy in copies:
+        copy.wait_recv()
+    width, tokens = got.shape[2], got.shape[3]
+    for source in range(frames):
+        span = slice(source * tokens, (source + 1) * tokens)
+        keys[span, :] = got[0, source].astype(F32).T.astype(BF16)
+        values[:, span] = got[2, source]
+    scale = 1.0 / math.sqrt(HD)
+    returns = []
+    for turn in range(1, frames + 1):
+        peer = lax.rem(frame + turn, frames)
+        for head in range(width // HD):
+            cols = slice(head * HD, (head + 1) * HD)
+            query = got[1, peer, cols, :]
+            scores = jnp.dot(keys[:, cols], query, preferred_element_type=F32) * scale
+            weights = jnp.exp(scores - jnp.max(scores, axis=0, keepdims=True))
+            denominator = jnp.sum(weights, axis=0, keepdims=True)
+            numerator = jnp.dot(
+                values[cols, :], weights.astype(BF16), preferred_element_type=F32
+            )
+            done[peer, cols, :] = (numerator / denominator).astype(BF16)
+        if turn < frames:
+            copy = remote(
+                done.at[peer],
+                back.at[frame],
+                out_send.at[turn],
+                out_recv.at[turn],
+                "frames",
+                peer,
+            )
+            copy.start()
+            returns.append(copy)
+    back[frame] = done[frame]
+    load.wait()
+    for copy in returns:
+        copy.wait_recv()
+    for source in range(frames):
+        att[:, source * width : (source + 1) * width] = (
+            back[source].astype(F32).T.astype(BF16)
+        )
+    size = hidden.shape[0]
+
+    def term(block):
+        rows = pl.ds(pl.multiple_of(block * size, size), size)
+        return jnp.dot(att[rows, :], weight[...], preferred_element_type=F32)
+
+    mixed = reduce_rows(term, sent, got_near, got_far, sum_send, sum_recv)
+    out_ref[...] = (hidden[...].astype(F32) + mixed).astype(BF16)
+    for copy in copies + returns:
+        copy.wait_send()
+
+
+def params(number):
+    return pltpu.CompilerParams(
+        collective_id=number, has_side_effects=True, vmem_limit_bytes=VMEM_LIMIT
+    )
+
+
+def sum_scratch(size, channels):
+    return [
+        pltpu.VMEM((3, size, channels), BF16),
+        pltpu.VMEM((2, size, channels), BF16),
+        pltpu.VMEM((size, channels), BF16),
+    ]
+
+
+def gather_rows(block):
+    peers = lax.axis_size("rows")
+    return pl.pallas_call(
+        gather_kernel,
+        out_shape=jax.ShapeDtypeStruct((peers,) + block.shape, block.dtype),
+        in_specs=[VMEM_SPEC],
+        out_specs=VMEM_SPEC,
+        scratch_shapes=[DMA((2 * PARTS + 1,)), DMA((2 * PARTS + 1,))],
+        compiler_params=params(0),
+    )(block)
+
+
+def temporal_normed(act, weight, latents, bias, gain):
+    peers, frames = lax.axis_size("rows"), lax.axis_size("frames")
+    size, channels = latents.shape
+    return pl.pallas_call(
+        functools.partial(temporal_kernel, frames),
+        out_shape=(
+            jax.ShapeDtypeStruct((size, channels), BF16),
+            jax.ShapeDtypeStruct((peers, size, channels), BF16),
+        ),
+        in_specs=[VMEM_SPEC, ANY_SPEC] + [VMEM_SPEC] * 3,
+        out_specs=(VMEM_SPEC, VMEM_SPEC),
+        scratch_shapes=[
+            pltpu.VMEM(weight.shape, BF16),
+            pltpu.VMEM((2,) + act.shape, BF16),
+            *sum_scratch(size, channels),
+            pltpu.VMEM((size, channels), BF16),
+            DMA,
+            DMA((2,)),
+            DMA((2,)),
+            DMA((3,)),
+            DMA((3,)),
+            DMA((2 * PARTS + 1,)),
+            DMA((2 * PARTS + 1,)),
+        ],
+        compiler_params=params(1),
+    )(act, weight, latents, bias.reshape(1, -1), gain.reshape(1, -1))
+
+
+def attended_mixed(queries, keys, values, weight, hidden):
+    frames = lax.axis_size("frames")
+    size, channels = hidden.shape
+    _, width, tokens = queries.shape
+    return pl.pallas_call(
+        functools.partial(attention_kernel, frames),
+        out_shape=jax.ShapeDtypeStruct((size, channels), BF16),
+        in_specs=[VMEM_SPEC] * 3 + [ANY_SPEC, VMEM_SPEC],
+        out_specs=VMEM_SPEC,
+        scratch_shapes=[
+            pltpu.VMEM(weight.shape, BF16),
+            pltpu.VMEM((3, frames, width, tokens), BF16),
+            pltpu.VMEM((frames * tokens, width), BF16),
+            pltpu.VMEM((width, frames * tokens), BF16),
+            pltpu.VMEM((frames, width, tokens), BF16),
+            pltpu.VMEM((frames, width, tokens), BF16),
+            pltpu.VMEM((tokens, frames * width), BF16),
+            *sum_scratch(size, channels),
+            DMA,
+            DMA((3, frames)),
+            DMA((3, frames)),
+            DMA((frames,)),
+            DMA((frames,)),
+            DMA((3,)),
+            DMA((3,)),
+        ],
+        compiler_params=params(2),
+    )(queries, keys, values, weight, hidden)
+
+
+def activate(plane, spatial_weight, spatial_bias, norm_gain, norm_shift):
+    plane_rows, frame_count, width_cells, _ = plane.shape
+    local_out = spatial_weight.shape[3]
+    spatial = conv_plane(plane, spatial_weight, spatial_bias)
+    local_groups = NORM_GROUPS // lax.axis_size("rows")
+    grouped = spatial.reshape(plane_rows, frame_count, width_cells, local_groups, -1)
+    group_mean = jnp.mean(grouped, axis=(0, 2, 4), keepdims=True)
+    centred = grouped - group_mean
+    group_var = jnp.mean(centred * centred, axis=(0, 2, 4), keepdims=True)
+    scaled = (centred / jnp.sqrt(group_var + 1e-05)).reshape(
+        plane_rows, frame_count, width_cells, local_out
+    ) * norm_gain + norm_shift
+    return jax.nn.silu(scaled).astype(jnp.bfloat16)
+
+
+def body_fast(
+    latents,
+    spatial_weight,
+    spatial_bias,
+    norm_gain,
+    norm_shift,
+    temporal_weight,
+    temporal_bias,
+    token_gain,
+    query_weight,
+    key_weight,
+    value_weight,
+    output_weight,
+):
+    row_count, frame_count, width_cells, channels = latents.shape
+    peers, frames = lax.axis_size("rows"), lax.axis_size("frames")
+    block = latents.reshape(-1, channels)
+    plane = gather_rows(block).reshape(peers * row_count, frame_count, width_cells, channels)
+    activated = activate(plane, spatial_weight, spatial_bias, norm_gain, norm_shift)
+    hidden, normed_all = temporal_normed(
+        activated.reshape(-1, activated.shape[3]),
+        temporal_weight,
+        block,
+        temporal_bias,
+        token_gain,
+    )
+    flat = normed_all.reshape(-1, channels)
+
+    def project(weight):
+        cols = lax.dot_general(
+            weight, flat, (((0,), (1,)), ((), ())), preferred_element_type=F32
+        ).astype(BF16)
+        return cols.reshape(frames, -1, flat.shape[0])
+
+    denoised = attended_mixed(
+        project(query_weight), project(key_weight), project(value_weight), output_weight, hidden
+    )
+    return denoised.reshape(latents.shape)
+
+
+def fits(mesh):
+    def choose(*args):
+        latents, query_weight = args[0], args[8]
+        peers, frames = mesh.shape["rows"], mesh.shape["frames"]
+        heads = query_weight.shape[1] // HD
+        tokens = latents.shape[0] * latents.shape[1] * latents.shape[2] * peers
+        fast = (
+            peers == 4
+            and latents.shape[1] == 1
+            and heads % frames == 0
+            and tokens % 128 == 0
+        )
+        return (body_fast if fast else body)(*args)
+
+    return choose
+
+
 def solution(mesh):
     in_specs = (
         P("rows", ("groups", "frames"), None, None),
@@ -190,4 +667,6 @@
         P("rows", None),
     )
     out_specs = P("rows", ("groups", "frames"), None, None)
-    return jax.shard_map(body, mesh=mesh, in_specs=in_specs, out_specs=out_specs, check_vma=False)
+    return jax.shard_map(
+        fits(mesh), mesh=mesh, in_specs=in_specs, out_specs=out_specs, check_vma=False
+    )

time: 144 us -> 84.3 us (0.59)
  waiting for transfers between devices: 63.8 us -> 0 us
  Pallas kernels: 0 us -> 56.5 us
  starting transfers between devices: 26 us -> 0 us
  blocking collectives: 17 us -> 0 us
  between operations: 13.7 us -> 0.27 us
  local copies, waits for them, and re-layouts: 2.77 us -> 8.07 us
  other arithmetic: 4.55 us -> 0.48 us
  matrix products: 15.3 us -> 18.5 us
    pallas_call x0 -> x3, Pallas kernels: none -> 56.5 us  [the longest x1 25.6 us: attended_mixed(): pl.pallas_call(functools.partial(attention_kernel, frames), out_shape=jax...]
    reduce_scatter x2 -> x0, waiting for transfers between devices: 44.7 us -> none  [the longest x1 24.3 us: body(): lax.psum_scatter(total.reshape(row_total, frame_count, width_cells, chann...]
    ppermute x18 -> x0, starting transfers between devices: 25.9 us -> none  [the longest x16 20 us: shifted_2(): return lax.ppermute(value, axis, pairs)]
    ppermute x18 -> x0, waiting for transfers between devices: 19.1 us -> none  [the longest x16 17.2 us: shifted_2(): return lax.ppermute(value, axis, pairs)]
    all_gather x2 -> x0, blocking collectives: 17 us -> none  [the longest x1 9.69 us: body(): plane = lax.all_gather(latents, 'rows', axis=0, tiled=True)]
    dot_general x9, matrix products: 5.55 us -> 16.2 us  [conv_plane(): jnp.dot(window, weight[row_off, col_off], preferred_element_type=jnp.floa...]
    dot_general x15 -> x3, matrix products: 9.79 us -> 2.27 us  [project(): lax.dot_general(weight, flat, (((0,), (1,)), ((), ())), preferred_element...]
    unnamed x24 -> x25, local copies, waits for them, and re-layouts: 0.26 us -> 3.4 us
  transfers between devices with their start and end apart: 20 -> 0, of which waited for: 8 -> 0; matrix products, arithmetic and copies ran while one was open for 2% -> 0% of each run, Pallas kernels for 0% -> 0%
where the time goes in v1:
time: 84.3 us; the launch traced here: 83.8 us
  Pallas kernels  56.5 us (67%)
  matrix products  18.5 us (22%)
  local copies, waits for them, and re-layouts  8.07 us (10%)
    pallas_call x1, Pallas kernels, attended_mixed(): pl.pallas_call(functools.partial(attention_kernel, frames), out_shape=jax...  25.6 us
    pallas_call x1, Pallas kernels, temporal_normed(): pl.pallas_call(functools.partial(temporal_kernel, frames), out_shape=(jax...  22.1 us
    dot_general x9, matrix products, conv_plane(): jnp.dot(window, weight[row_off, col_off], preferred_element_type=jnp.floa...  16.2 us
    pallas_call x1, Pallas kernels, gather_rows(): pl.pallas_call(gather_kernel, out_shape=jax.ShapeDtypeStruct((peers,) + b...  8.85 us
    unnamed x25, local copies, waits for them, and re-layouts  3.4 us
    dot_general x3, matrix products, project(): lax.dot_general(weight, flat, (((0,), (1,)), ((), ())), preferred_element...  2.27 us
    slice x1, local copies, waits for them, and re-layouts, conv_plane(): padded[row_off:row_off + rows_n, :, col_off:col_off + cols_n, :]  2.25 us
    add x1, local copies, waits for them, and re-layouts, conv_plane(): total + jnp.dot(window, weight[row_off, col_off], preferred_element_type=...  1.94 us

profile of v1, /device:TPU:0, one launch (start us, length us, event | category | flops | bytes accessed | tf_op | source)
XLA Modules:
  0.0 83.8 jit_solution(5914509049521439223)
XLA Ops:
  0.0 1.0 %copy-done.2 = bf16[4,1,16,1280]{3,2,1,0:T(8,128)(2,1)S(1)} copy-done((bf16[4,1,16,1280]{3,2,1,0:T(8,128)(2,1)S(1)}, bf16[4,1,16,1280]{3,2,1,0:T(8,128)(2,1)}, u32[]{:S(2)}) %copy-start.2) | copy-done | bytes 163864
  1.0 8.8 %shard_map.118 = bf16[4,64,1280]{2,1,0:T(8,128)(2,1)S(1)} custom-call(bf16[64,1280]{1,0:T(8,128)(2,1)S(1)} %bitcast.73), custom_call_target="tpu_custom_call" | custom-call | tf_op jit(solution)/shard_map/pallas_call | solution.py:514
  9.8 2.3 %pad_slice_fusion = (bf16[16,1,16,1280]{3,2,0,1:T(8,128)(2,1)}, bf16[16,1,16,1280]{3,2,0,1:T(8,128)(2,1)S(1)}, bf16[16,1,16,1280]{3,2,0,1:T(8,128)(2,1)}, bf16[1...) fusion(bf16[16,1,16,1280]{3,2,0,1:T(8,128)(2,1)S(1)} %bitcast.71), kind=kLoop, calls=%fused_computation | loop fusion | bytes 5898240 | tf_op jit(solution)/shard_map/slice | solution.py:40
  12.1 1.5 %fusion.9 = f32[256,320]{0,1:T(8,128)S(1)} fusion(bf16[256,1280]{1,0:T(8,128)(2,1)S(1)} %bitcast.86, bf16[3,3,1280,320]{2,3,1,0:T(8,128)(2,1)} %param.13), kind=kOutput, calls=%fused_computation.28 | convolution fusion | flops 209715200 | bytes 1802240 | tf_op jit(solution)/shard_map/dot_general | solution.py:43
  13.6 2.3 %convolution_add_fusion.7 = f32[256,320]{0,1:T(8,128)} fusion(f32[256,320]{0,1:T(8,128)S(1)} %fusion.9, bf16[256,1280]{1,0:T(8,128)(2,1)S(1)} %bitcast.79, bf16[3,3,1280,320]{2,3,1,0:T(8,128)(2,1)} %param.13), kind=kOutput, calls=%fused_computation.16 | convolution fusion | flops 209797120 | bytes 2129920 | tf_op jit(solution)/shard_map/dot_general | solution.py:43
  15.9 1.9 %copy.33 = f32[256,320]{1,0:T(8,128)} copy(f32[256,320]{0,1:T(8,128)} %convolution_add_fusion.7) | data formatting | bytes 655360 | tf_op jit(solution)/shard_map/add | solution.py:43
  17.9 2.0 %convolution_add_fusion.6 = f32[256,320]{1,0:T(8,128)S(1)} fusion(f32[256,320]{1,0:T(8,128)} %copy.33, bf16[256,1280]{1,0:T(8,128)(2,1)} %bitcast.84, bf16[3,3,1280,320]{2,3,1,0:T(8,128)(2,1)} %param.13), kind=kOutput, calls=%fused_computation.15 | convolution fusion | flops 209797120 | bytes 2195456 | tf_op jit(solution)/shard_map/dot_general | solution.py:43
  19.9 0.0 copy-start.9
  20.0 1.9 %convolution_add_fusion.5 = f32[256,320]{1,0:T(8,128)S(1)} fusion(f32[256,320]{1,0:T(8,128)S(1)} %convolution_add_fusion.6, bf16[256,1280]{1,0:T(8,128)(2,1)} %bitcast.83, bf16[3,3,1280,320]{2,3,1,0:T(8,128)(2,1)} %param.13), kind=kOutput, calls=%fused_computation.14 | convolution fusion | flops 209797120 | bytes 2129920 | tf_op jit(solution)/shard_map/dot_general | solution.py:43
  21.9 1.7 %convolution_add_fusion.4 = f32[256,320]{1,0:T(8,128)S(1)} fusion(f32[256,320]{1,0:T(8,128)S(1)} %convolution_add_fusion.5, bf16[256,1280]{1,0:T(8,128)(2,1)S(1)} %bitcast.72, bf16[3,3,1280,320]{2,3,1,0:T(8,128)(2,1)} %param.13), kind=kOutput, calls=%fused_computation.13 | convolution fusion | flops 209797120 | bytes 2129920 | tf_op jit(solution)/shard_map/dot_general | solution.py:43
  23.6 1.7 %convolution_add_fusion.3 = f32[256,320]{1,0:T(8,128)S(1)} fusion(f32[256,320]{1,0:T(8,128)S(1)} %convolution_add_fusion.4, bf16[256,1280]{1,0:T(8,128)(2,1)S(1)} %bitcast.82, bf16[3,3,1280,320]{2,3,1,0:T(8,128)(2,1)} %param.13), kind=kOutput, calls=%fused_computation.12 | convolution fusion | flops 209797120 | bytes 2129920 | tf_op jit(solution)/shard_map/dot_general | solution.py:43
  25.3 1.7 %convolution_add_fusion.2 = f32[256,320]{1,0:T(8,128)S(1)} fusion(f32[256,320]{1,0:T(8,128)S(1)} %convolution_add_fusion.3, bf16[256,1280]{1,0:T(8,128)(2,1)S(1)} %bitcast.81, bf16[3,3,1280,320]{2,3,1,0:T(8,128)(2,1)} %param.13), kind=kOutput, calls=%fused_computation.11 | convolution fusion | flops 209797120 | bytes 2129920 | tf_op jit(solution)/shard_map/dot_general | solution.py:43
  27.1 1.7 %convolution_add_fusion.1 = f32[256,320]{1,0:T(8,128)S(1)} fusion(f32[256,320]{1,0:T(8,128)S(1)} %convolution_add_fusion.2, bf16[256,1280]{1,0:T(8,128)(2,1)S(1)} %bitcast.80, bf16[3,3,1280,320]{2,3,1,0:T(8,128)(2,1)} %param.13), kind=kOutput, calls=%fused_computation.10 | convolution fusion | flops 209797120 | bytes 2129920 | tf_op jit(solution)/shard_map/dot_general | solution.py:43
  28.8 1.7 %fusion.20 = (f32[320]{0:T(512)S(1)}, f32[256,320]{1,0:T(8,128)S(1)}) fusion(f32[320]{0:T(512)S(1)} %copy-done.11, f32[256,320]{1,0:T(8,128)S(1)} %convolution_add_fusion.1, bf16[256,1280]{1,0:T(8,128)(2,1)S(1)} %bitcast.85, bf16[3,3,1280,320]{2,3,1,0:T(8,128)(2,1)} %param.13), kind=kOutput, calls=%fused_computation.43 | convolution fusion | flops 209960640 | bytes 2132480 | tf_op jit(solution)/shard_map/dot_general | solution.py:43
  30.5 0.1 reduce_sum.24
  30.5 0.1 reduce_sum.25
  30.7 0.1 sub.21
  30.7 0.1 sub.22
  30.8 0.1 multiply_reduce_fusion
  30.9 0.1 reduce_sum.36
  31.0 0.1 reduce_sum.37
  31.1 0.1 div.32
  31.2 0.1 div.33
  31.3 0.0 copy-done.9
  31.3 0.1 multiply_convert_fusion.act
  31.5 1.7 %copy-done.1 = bf16[3,320,1280]{2,1,0:T(8,128)(2,1)S(1)} copy-done((bf16[3,320,1280]{2,1,0:T(8,128)(2,1)S(1)}, bf16[3,320,1280]{2,1,0:T(8,128)(2,1)}, u32[]{:S(2)}) %copy-start.1) | copy-done | bytes 2457624
  33.2 22.1 %shard_map.119 = (bf16[64,1280]{1,0:T(8,128)(2,1)S(1)}, bf16[4,64,1280]{2,1,0:T(8,128)(2,1)S(1)}) custom-call(bf16[256,320]{1,0:T(8,128)(2,1)S(1)} %multiply_convert_fusion.act, bf16[3,320,1280]{2,1,0:T(8,128)(2,1)S(1)} %copy-done.1, bf16[64,1280]{1,0:T(8,128)(2,1)S(1)} %bitcast.74, f32[1,1280]{1,0:T(1,128)S(1)} %reshape.143.bias, f32[1,1280]{1,0:T(1,128)S(1)} %reshape.144.gain), custom_call_target="tpu_custom_call" | custom-call | tf_op jit(solution)/shard_map/pallas_call | solution.py:527
  55.3 0.4 convolution_convert_fusion.2
  55.7 0.4 convolution_convert_fusion.1
  56.1 1.5 %convolution_convert_fusion = bf16[256,256]{0,1:T(8,128)(2,1)S(1)} fusion(bf16[256,1280]{1,0:T(8,128)(2,1)S(1)} %bitcast.70, bf16[1280,256]{1,0:T(8,128)(2,1)} %param.22), kind=kOutput, calls=%fused_computation.17 | convolution fusion | flops 167837696 | bytes 1441792 | tf_op jit(solution)/shard_map/dot_general | solution.py:626
  57.6 25.6 %shard_map.120 = bf16[64,1280]{1,0:T(8,128)(2,1)S(1)} custom-call(bf16[4,64,256]{2,1,0:T(8,128)(2,1)S(1)} %bitcast.76, bf16[4,64,256]{2,1,0:T(8,128)(2,1)S(1)} %bitcast.77, bf16[4,64,256]{2,1,0:T(8,128)(2,1)S(1)} %bitcast.78, bf16[256,1280]{1,0:T(8,128)(2,1)S(1)} %copy-done.4, bf16[64,1280]{1,0:T(8,128)(2,1)S(1)} %get-tuple-element.8.hidden), custom_call_target="tpu_custom_call" | custom-call | tf_op jit(solution)/shard_map/pallas_call | solution.py:556
  83.1 0.7 copy.50
  (24 shorter events, 0.1 us)
Async XLA Ops:
  0.0 55.3 %copy-start = (bf16[1280,256]{1,0:T(8,128)(2,1)S(1)}, bf16[1280,256]{1,0:T(8,128)(2,1)}, u32[]{:S(2)}) copy-start(bf16[1280,256]{1,0:T(8,128)(2,1)} %param.20) | copy-start | bytes 1966084
  0.0 1.0 %copy-start.2 = (bf16[4,1,16,1280]{3,2,1,0:T(8,128)(2,1)S(1)}, bf16[4,1,16,1280]{3,2,1,0:T(8,128)(2,1)}, u32[]{:S(2)}) copy-start(bf16[4,1,16,1280]{3,2,1,0:T(8,128)(2,1)} %param.12) | copy-start | bytes 491524
  15.9 12.8 %copy-start.11 = (f32[320]{0:T(512)S(1)}, f32[320]{0:T(512)}, u32[]{:S(2)}) copy-start(f32[320]{0:T(512)} %param.14) | copy-start | bytes 3844
  17.9 10.9 %copy-start.6 = (bf16[16,1,16,1280]{3,2,0,1:T(8,128)(2,1)S(1)}, bf16[16,1,16,1280]{3,2,0,1:T(8,128)(2,1)}, u32[]{:S(2)}) copy-start(bf16[16,1,16,1280]{3,2,0,1:T(8,128)(2,1)} %get-tuple-element.9) | copy-start | bytes 1966084
  19.9 11.4 %copy-start.9 = (f32[320]{0:T(512)S(1)}, f32[320]{0:T(512)}, u32[]{:S(2)}) copy-start(f32[320]{0:T(512)} %param.16) | copy-start | bytes 3844
  19.9 11.4 %copy-start.10 = (f32[320]{0:T(512)S(1)}, f32[320]{0:T(512)}, u32[]{:S(2)}) copy-start(f32[320]{0:T(512)} %param.15) | copy-start | bytes 3844
  19.9 11.5 %copy-start.7 = (f32[1280]{0:T(1024)S(1)}, f32[1280]{0:T(1024)}, u32[]{:S(2)}) copy-start(f32[1280]{0:T(1024)} %param.18) | copy-start | bytes 15364
  20.0 11.5 %copy-start.8 = (f32[1280]{0:T(1024)S(1)}, f32[1280]{0:T(1024)}, u32[]{:S(2)}) copy-start(f32[1280]{0:T(1024)} %param.19) | copy-start | bytes 15364
  20.0 11.5 %copy-start.3 = (bf16[4,1,16,1280]{3,2,1,0:T(8,128)(2,1)S(1)}, bf16[4,1,16,1280]{3,2,1,0:T(8,128)(2,1)}, u32[]{:S(2)}) copy-start(bf16[4,1,16,1280]{3,2,1,0:T(8,128)(2,1)} %param.12) | copy-start | bytes 491524
  23.6 32.1 %copy-start.5 = (bf16[1280,256]{1,0:T(8,128)(2,1)S(1)}, bf16[1280,256]{1,0:T(8,128)(2,1)}, u32[]{:S(2)}) copy-start(bf16[1280,256]{1,0:T(8,128)(2,1)} %param.21) | copy-start | bytes 1966084
  25.3 32.3 %copy-start.4 = (bf16[256,1280]{1,0:T(8,128)(2,1)S(1)}, bf16[256,1280]{1,0:T(8,128)(2,1)}, u32[]{:S(2)}) copy-start(bf16[256,1280]{1,0:T(8,128)(2,1)} %weight_hbm.3) | copy-start | bytes 1966084
  31.5 1.7 %copy-start.1 = (bf16[3,320,1280]{2,1,0:T(8,128)(2,1)S(1)}, bf16[3,320,1280]{2,1,0:T(8,128)(2,1)}, u32[]{:S(2)}) copy-start(bf16[3,320,1280]{2,1,0:T(8,128)(2,1)} %weight_hbm.2) | copy-start | bytes 7372804

commit v2 on v0

--- a/solution.py
+++ b/solution.py
@@ -1,8 +1,11 @@
+import functools
 import math
 
 import jax
 import jax.numpy as jnp
 from jax import lax
+from jax.experimental import pallas as pl
+from jax.experimental.pallas import tpu as pltpu
 from jax.sharding import PartitionSpec as P
 
 HD = 64
@@ -174,6 +177,520 @@
     return (hidden.astype(jnp.float32) + mixed).astype(jnp.bfloat16)
 
 
+MESH = pl.DeviceIdType.MESH
+DMA = pltpu.SemaphoreType.DMA
+VMEM_SPEC = pl.BlockSpec(memory_space=pltpu.VMEM)
+ANY_SPEC = pl.BlockSpec(memory_space=pl.ANY)
+BF16 = jnp.bfloat16
+F32 = jnp.float32
+VMEM_LIMIT = 56 << 20
+PARTS = 2
+
+
+def remote(src, dst, send, recv, axis, peer):
+    return pltpu.make_async_remote_copy(
+        src_ref=src,
+        dst_ref=dst,
+        send_sem=send,
+        recv_sem=recv,
+        device_id={axis: peer},
+        device_id_type=MESH,
+    )
+
+
+def greet(barrier, axis, peer):
+    pl.semaphore_signal(barrier, inc=1, device_id={axis: peer}, device_id_type=MESH)
+
+
+class Gather:
+    def __init__(self, block, out, send, recv):
+        me = lax.axis_index("rows")
+        near, far = me ^ 1, me ^ 2
+        step = block.shape[0] // PARTS
+        self.far, self.onward = [], []
+        for part in range(PARTS):
+            piece = pl.ds(part * step, step)
+            self.far.append(
+                remote(
+                    block.at[piece],
+                    out.at[me, piece],
+                    send.at[part],
+                    recv.at[part],
+                    "rows",
+                    far,
+                )
+            )
+            self.onward.append(
+                remote(
+                    out.at[far, piece],
+                    out.at[far, piece],
+                    send.at[PARTS + part],
+                    recv.at[PARTS + part],
+                    "rows",
+                    near,
+                )
+            )
+        self.near = remote(
+            block, out.at[me], send.at[2 * PARTS], recv.at[2 * PARTS], "rows", near
+        )
+
+    def start(self):
+        for copy in self.far:
+            copy.start()
+        self.near.start()
+
+    def finish(self):
+        for copy, onward in zip(self.far, self.onward):
+            copy.wait_recv()
+            onward.start()
+        for copy in self.far:
+            copy.wait_send()
+        self.near.wait()
+        for onward in self.onward:
+            onward.wait()
+
+
+def reduce_rows(term, sent, got_near, got_far, send, recv):
+    me = lax.axis_index("rows")
+    near, far = me ^ 1, me ^ 2
+
+    def hand(slot, value):
+        sent[slot] = value.astype(BF16)
+        copy = remote(
+            sent.at[slot], got_near.at[slot], send.at[slot], recv.at[slot], "rows", near
+        )
+        copy.start()
+        return copy
+
+    first = hand(0, term(far ^ 1, 0))
+    mine = term(far, 1)
+    first.wait_recv()
+    sent[2] = (mine + got_near[0].astype(F32)).astype(BF16)
+    across = remote(sent.at[2], got_far, send.at[2], recv.at[2], "rows", far)
+    across.start()
+    second = hand(1, term(near, 2))
+    mine = term(me, 3)
+    second.wait_recv()
+    mine = mine + got_near[1].astype(F32)
+    across.wait_recv()
+    total = mine + got_far[...].astype(F32)
+    for copy in (first, second, across):
+        copy.wait_send()
+    return total
+
+
+def convolve(plane, shifted, weight, width):
+    blocks, size, channels = plane.shape
+    tokens = blocks * size
+    edge = jnp.zeros((width, channels), BF16)
+    column = lax.broadcasted_iota(jnp.int32, (size, channels), 0) % width
+    for offset in range(3):
+        shifted[offset, :width, :] = edge
+        shifted[offset, tokens + width :, :] = edge
+    for block in range(blocks):
+        rows = slice(width + block * size, width + (block + 1) * size)
+        value = plane[block]
+        wide = value.astype(F32)
+        before = jnp.where(column == 0, 0.0, pltpu.roll(wide, 1, 0))
+        after = jnp.where(column == width - 1, 0.0, pltpu.roll(wide, size - 1, 0))
+        shifted[0, rows, :] = before.astype(BF16)
+        shifted[1, rows, :] = value
+        shifted[2, rows, :] = after.astype(BF16)
+    total = None
+    for row_off in range(3):
+        for col_off in range(3):
+            window = shifted[col_off, row_off * width : row_off * width + tokens, :]
+            part = jnp.dot(window, weight[row_off, col_off], preferred_element_type=F32)
+            total = part if total is None else total + part
+    return total
+
+
+def group_norm_silu(spatial, gain, shift, groups):
+    tokens, channels = spatial.shape
+    per = channels // groups
+    lane = lax.broadcasted_iota(jnp.int32, (groups, channels), 1)
+    first = lax.broadcasted_iota(jnp.int32, (groups, channels), 0) * per
+    member = jnp.logical_and(lane >= first, lane < first + per)
+
+    def group_mean(value):
+        column = jnp.sum(value, axis=0, keepdims=True)
+        sums = jnp.sum(jnp.where(member, column, 0.0), axis=1, keepdims=True)
+        return jnp.sum(jnp.where(member, sums, 0.0), axis=0, keepdims=True) / (tokens * per)
+
+    centred = spatial - group_mean(spatial)
+    scale = 1.0 / jnp.sqrt(group_mean(centred * centred) + 1e-05)
+    value = centred * scale * gain + shift
+    return (value / (1.0 + jnp.exp(-value))).astype(BF16)
+
+
+def block_kernel(
+    frames,
+    width_cells,
+    groups,
+    latents_hbm,
+    spatial_hbm,
+    spatial_bias,
+    norm_gain,
+    norm_shift,
+    temporal_hbm,
+    temporal_bias,
+    token_gain,
+    query_hbm,
+    key_hbm,
+    value_hbm,
+    output_hbm,
+    out_ref,
+    latents,
+    spatial_w,
+    temporal_w,
+    project_w,
+    output_w,
+    plane,
+    shifted,
+    act,
+    halo,
+    normed,
+    normed_all,
+    outgoing,
+    got,
+    keys,
+    values,
+    probs,
+    done,
+    back,
+    att,
+    sent,
+    got_near,
+    got_far,
+    load_sem,
+    lat_send,
+    lat_recv,
+    halo_send,
+    halo_recv,
+    gat_send,
+    gat_recv,
+    in_send,
+    in_recv,
+    out_send,
+    out_recv,
+    sum_send,
+    sum_recv,
+):
+    me = lax.axis_index("rows")
+    frame = lax.axis_index("frames")
+    near, far = me ^ 1, me ^ 2
+    loads = []
+    for index, (src, dst) in enumerate(
+        (
+            (latents_hbm, latents),
+            (spatial_hbm, spatial_w),
+            (temporal_hbm, temporal_w),
+            (key_hbm, project_w.at[0]),
+            (query_hbm, project_w.at[1]),
+            (value_hbm, project_w.at[2]),
+            (output_hbm, output_w),
+        )
+    ):
+        load = pltpu.make_async_copy(src, dst, load_sem.at[index])
+        load.start()
+        loads.append(load)
+    barrier = pltpu.get_barrier_semaphore()
+    greet(barrier, "rows", near)
+    greet(barrier, "rows", far)
+    for turn in range(1, frames):
+        greet(barrier, "frames", lax.rem(frame + turn, frames))
+    pl.semaphore_wait(barrier, frames + 1)
+
+    loads[0].wait()
+    gather = Gather(latents, plane, lat_send, lat_recv)
+    gather.start()
+    plane[me] = latents[...]
+    gather.finish()
+    loads[1].wait()
+    spatial = convolve(plane, shifted, spatial_w, width_cells) + spatial_bias[...]
+    act[...] = group_norm_silu(spatial, norm_gain[...], norm_shift[...], groups)
+
+    has_prev, has_next = frame > 0, frame < frames - 1
+    prev = jnp.maximum(frame - 1, 0)
+    later = jnp.minimum(frame + 1, frames - 1)
+    size = latents.shape[0]
+
+    def rows_of(block):
+        return pl.ds(pl.multiple_of(block * size, size), size)
+
+    up, down = [], []
+    for turn, block in enumerate((far ^ 1, far, near, me)):
+        rows = rows_of(block)
+        for side, (copies, peer) in enumerate(((up, later), (down, prev))):
+            copies.append(
+                remote(
+                    act.at[rows],
+                    halo.at[side, rows],
+                    halo_send.at[side, turn],
+                    halo_recv.at[side, turn],
+                    "frames",
+                    peer,
+                )
+            )
+
+    @pl.when(has_next)
+    def _():
+        for copy in up:
+            copy.start()
+
+    @pl.when(has_prev)
+    def _():
+        for copy in down:
+            copy.start()
+
+    @pl.when(jnp.logical_not(has_prev))
+    def _():
+        halo[0] = jnp.zeros(halo.shape[1:], halo.dtype)
+
+    @pl.when(jnp.logical_not(has_next))
+    def _():
+        halo[1] = jnp.zeros(halo.shape[1:], halo.dtype)
+
+    loads[2].wait()
+
+    def temporal_term(block, turn):
+        rows = rows_of(block)
+        total = jnp.dot(act[rows, :], temporal_w[1], preferred_element_type=F32)
+
+        @pl.when(has_prev)
+        def _():
+            up[turn].wait_recv()
+
+        @pl.when(has_next)
+        def _():
+            down[turn].wait_recv()
+
+        total += jnp.dot(halo[0, rows, :], temporal_w[0], preferred_element_type=F32)
+        total += jnp.dot(halo[1, rows, :], temporal_w[2], preferred_element_type=F32)
+        return total
+
+    temporal = reduce_rows(
+        temporal_term, sent.at[0], got_near.at[0], got_far.at[0], sum_send.at[0], sum_recv.at[0]
+    )
+
+    @pl.when(has_next)
+    def _():
+        for copy in up:
+            copy.wait_send()
+
+    @pl.when(has_prev)
+    def _():
+        for copy in down:
+            copy.wait_send()
+
+    hidden = (latents[...].astype(F32) + temporal + temporal_bias[...]).astype(BF16)
+    flat = hidden.astype(F32)
+    centred = flat - jnp.mean(flat, axis=-1, keepdims=True)
+    var = jnp.mean(centred * centred, axis=-1, keepdims=True)
+    normed[...] = (centred / jnp.sqrt(var + 1e-05) * token_gain[...]).astype(BF16)
+    gather = Gather(normed, normed_all, gat_send, gat_recv)
+    gather.start()
+    normed_all[me] = normed[...]
+    gather.finish()
+
+    tokens = act.shape[0]
+    width = got.shape[2]
+    tokens_in = normed_all[...].reshape(tokens, -1)
+    moves = []
+    for kind in range(3):
+        loads[3 + kind].wait()
+        cols = jnp.dot(tokens_in, project_w[kind], preferred_element_type=F32)
+        cols = cols.T.astype(BF16)
+        for owner in range(frames):
+            outgoing[kind, owner] = cols[owner * width : (owner + 1) * width, :]
+        batch = []
+        for turn in range(1, frames):
+            peer = lax.rem(frame + turn, frames)
+            copy = remote(
+                outgoing.at[kind, peer],
+                got.at[kind, frame],
+                in_send.at[kind, turn],
+                in_recv.at[kind, turn],
+                "frames",
+                peer,
+            )
+            copy.start()
+            batch.append(copy)
+        got[kind, frame] = outgoing[kind, frame]
+        moves.append(batch)
+
+    for copy in moves[0]:
+        copy.wait_recv()
+    for source in range(frames):
+        span = slice(source * tokens, (source + 1) * tokens)
+        keys[span, :] = got[0, source].astype(F32).T.astype(BF16)
+    for copy in moves[1]:
+        copy.wait_recv()
+    scale = 1.0 / math.sqrt(HD)
+    heads = width // HD
+    sums = []
+    for turn in range(1, frames + 1):
+        peer = lax.rem(frame + turn, frames)
+        for head in range(heads):
+            cols = slice(head * HD, (head + 1) * HD)
+            query = got[1, peer, cols, :]
+            scores = jnp.dot(keys[:, cols], query, preferred_element_type=F32) * scale
+            weights = jnp.exp(scores - jnp.max(scores, axis=0, keepdims=True))
+            sums.append(jnp.sum(weights, axis=0, keepdims=True))
+            probs[(turn - 1) * heads + head] = weights.astype(BF16)
+    for copy in moves[2]:
+        copy.wait_recv()
+    for source in range(frames):
+        values[:, source * tokens : (source + 1) * tokens] = got[2, source]
+    returns = []
+    for turn in range(1, frames + 1):
+        peer = lax.rem(frame + turn, frames)
+        for head in range(heads):
+            cols = slice(head * HD, (head + 1) * HD)
+            place = (turn - 1) * heads + head
+            numerator = jnp.dot(values[cols, :], probs[place], preferred_element_type=F32)
+            done[peer, cols, :] = (numerator / sums[place]).astype(BF16)
+        if turn < frames:
+            copy = remote(
+                done.at[peer],
+                back.at[frame],
+                out_send.at[turn],
+                out_recv.at[turn],
+                "frames",
+                peer,
+            )
+            copy.start()
+            returns.append(copy)
+    back[frame] = done[frame]
+    loads[6].wait()
+    for copy in returns:
+        copy.wait_recv()
+    for source in range(frames):
+        att[:, source * width : (source + 1) * width] = (
+            back[source].astype(F32).T.astype(BF16)
+        )
+
+    def mixed_term(block, turn):
+        return jnp.dot(att[rows_of(block), :], output_w[...], preferred_element_type=F32)
+
+    mixed = reduce_rows(
+        mixed_term, sent.at[1], got_near.at[1], got_far.at[1], sum_send.at[1], sum_recv.at[1]
+    )
+    out_ref[...] = (hidden.astype(F32) + mixed).astype(BF16)
+    for batch in moves + [returns]:
+        for copy in batch:
+            copy.wait_send()
+
+
+def body_fast(
+    latents,
+    spatial_weight,
+    spatial_bias,
+    norm_gain,
+    norm_shift,
+    temporal_weight,
+    temporal_bias,
+    token_gain,
+    query_weight,
+    key_weight,
+    value_weight,
+    output_weight,
+):
+    channels = latents.shape[3]
+    peers, frames = lax.axis_size("rows"), lax.axis_size("frames")
+    block = latents.reshape(-1, channels)
+    size = block.shape[0]
+    tokens = size * peers
+    width_cells = latents.shape[2]
+    local_out = spatial_weight.shape[3]
+    width = query_weight.shape[1] // frames
+    heads = width // HD
+    links = 2 * PARTS + 1
+    denoised = pl.pallas_call(
+        functools.partial(block_kernel, frames, width_cells, NORM_GROUPS // peers),
+        out_shape=jax.ShapeDtypeStruct(block.shape, BF16),
+        in_specs=[ANY_SPEC] * 2
+        + [VMEM_SPEC] * 3
+        + [ANY_SPEC]
+        + [VMEM_SPEC] * 2
+        + [ANY_SPEC] * 4,
+        out_specs=VMEM_SPEC,
+        scratch_shapes=[
+            pltpu.VMEM(block.shape, BF16),
+            pltpu.VMEM(spatial_weight.shape, BF16),
+            pltpu.VMEM(temporal_weight.shape, BF16),
+            pltpu.VMEM((3,) + query_weight.shape, BF16),
+            pltpu.VMEM(output_weight.shape, BF16),
+            pltpu.VMEM((peers,) + block.shape, BF16),
+            pltpu.VMEM((3, tokens + 2 * width_cells, channels), BF16),
+            pltpu.VMEM((tokens, local_out), BF16),
+            pltpu.VMEM((2, tokens, local_out), BF16),
+            pltpu.VMEM(block.shape, BF16),
+            pltpu.VMEM((peers,) + block.shape, BF16),
+            pltpu.VMEM((3, frames, width, tokens), BF16),
+            pltpu.VMEM((3, frames, width, tokens), BF16),
+            pltpu.VMEM((frames * tokens, width), BF16),
+            pltpu.VMEM((width, frames * tokens), BF16),
+            pltpu.VMEM((frames * heads, frames * tokens, tokens), BF16),
+            pltpu.VMEM((frames, width, tokens), BF16),
+            pltpu.VMEM((frames, width, tokens), BF16),
+            pltpu.VMEM((tokens, frames * width), BF16),
+            pltpu.VMEM((2, 3) + block.shape, BF16),
+            pltpu.VMEM((2, 2) + block.shape, BF16),
+            pltpu.VMEM((2,) + block.shape, BF16),
+            DMA((7,)),
+            DMA((links,)),
+            DMA((links,)),
+            DMA((2, peers)),
+            DMA((2, peers)),
+            DMA((links,)),
+            DMA((links,)),
+            DMA((3, frames)),
+            DMA((3, frames)),
+            DMA((frames,)),
+            DMA((frames,)),
+            DMA((2, 3)),
+            DMA((2, 3)),
+        ],
+        compiler_params=pltpu.CompilerParams(
+            collective_id=0, has_side_effects=True, vmem_limit_bytes=VMEM_LIMIT
+        ),
+    )(
+        block,
+        spatial_weight,
+        spatial_bias.reshape(1, -1),
+        norm_gain.reshape(1, -1),
+        norm_shift.reshape(1, -1),
+        temporal_weight,
+        temporal_bias.reshape(1, -1),
+        token_gain.reshape(1, -1),
+        query_weight,
+        key_weight,
+        value_weight,
+        output_weight,
+    )
+    return denoised.reshape(latents.shape)
+
+
+def fits(mesh):
+    def choose(*args):
+        latents, query_weight = args[0], args[8]
+        peers, frames = mesh.shape["rows"], mesh.shape["frames"]
+        heads = query_weight.shape[1] // HD
+        tokens = latents.shape[0] * latents.shape[1] * latents.shape[2] * peers
+        fast = (
+            peers == 4
+            and latents.shape[1] == 1
+            and heads % frames == 0
+            and tokens % 128 == 0
+            and latents.shape[2] % 16 == 0
+            and latents.shape[0] * latents.shape[2] % (16 * PARTS) == 0
+        )
+        return (body_fast if fast else body)(*args)
+
+    return choose
+
+
 def solution(mesh):
     in_specs = (
         P("rows", ("groups", "frames"), None, None),
@@ -190,4 +707,6 @@
         P("rows", None),
     )
     out_specs = P("rows", ("groups", "frames"), None, None)
-    return jax.shard_map(body, mesh=mesh, in_specs=in_specs, out_specs=out_specs, check_vma=False)
+    return jax.shard_map(
+        fits(mesh), mesh=mesh, in_specs=in_specs, out_specs=out_specs, check_vma=False
+    )

time: 144 us -> 77.9 us (0.54)
  waiting for transfers between devices: 63.8 us -> 0 us
  Pallas kernels: 0 us -> 56.5 us
  starting transfers between devices: 26 us -> 0 us
  local copies, waits for them, and re-layouts: 2.77 us -> 20.8 us
  blocking collectives: 17 us -> 0 us
  matrix products: 15.3 us -> 0 us
  between operations: 13.7 us -> 0.01 us
  other arithmetic: 4.55 us -> 0 us
    pallas_call x0 -> x1, Pallas kernels: none -> 56.5 us  [body_fast(): pl.pallas_call(functools.partial(block_kernel, frames, width_cells, NORM_...]
    reduce_scatter x2 -> x0, waiting for transfers between devices: 44.7 us -> none  [the longest x1 24.3 us: body(): lax.psum_scatter(total.reshape(row_total, frame_count, width_cells, chann...]
    ppermute x18 -> x0, starting transfers between devices: 25.9 us -> none  [the longest x16 20 us: shifted_2(): return lax.ppermute(value, axis, pairs)]
    ppermute x18 -> x0, waiting for transfers between devices: 19.1 us -> none  [the longest x16 17.2 us: shifted_2(): return lax.ppermute(value, axis, pairs)]
    all_gather x2 -> x0, blocking collectives: 17 us -> none  [the longest x1 9.69 us: body(): plane = lax.all_gather(latents, 'rows', axis=0, tiled=True)]
    dot_general x24 -> x0, matrix products: 15.3 us -> none  [the longest x9 5.55 us: conv_plane(): jnp.dot(window, weight[row_off, col_off], preferred_element_type=jnp.floa...]
    unnamed x24 -> x2, local copies, waits for them, and re-layouts: 0.26 us -> 14.5 us
    reshape x0 -> x5, local copies, waits for them, and re-layouts: none -> 6.33 us  [the longest x1 1.3 us: body_fast(): token_gain.reshape(1, -1)]
  transfers between devices with their start and end apart: 20 -> 0, of which waited for: 8 -> 0; matrix products, arithmetic and copies ran while one was open for 2% -> 0% of each run, Pallas kernels for 0% -> 0%
where the time goes in v2:
time: 77.9 us; the launch traced here: 77.3 us
  Pallas kernels  56.5 us (73%)
  local copies, waits for them, and re-layouts  20.8 us (27%)
    pallas_call x1, Pallas kernels, body_fast(): pl.pallas_call(functools.partial(block_kernel, frames, width_cells, NORM_...  56.5 us
    unnamed x2, local copies, waits for them, and re-layouts  14.5 us

profile of v2, /device:TPU:0, one launch (start us, length us, event | category | flops | bytes accessed | tf_op | source)
XLA Modules:
  0.0 77.3 jit_solution(18051239360031788318)
XLA Ops:
  0.0 1.2 %reshape.22.spatial_bias = f32[1,320]{1,0:T(1,128)} reshape(f32[320]{0:T(512)} %param.14) | data formatting | bytes 2560 | tf_op jit(solution)/shard_map/reshape | solution.py:661
  1.2 1.3 %reshape.23.norm_gain = f32[1,320]{1,0:T(1,128)} reshape(f32[320]{0:T(512)} %param.15) | data formatting | bytes 2560 | tf_op jit(solution)/shard_map/reshape | solution.py:662
  2.5 1.3 %reshape.24.norm_shift = f32[1,320]{1,0:T(1,128)} reshape(f32[320]{0:T(512)} %param.16) | data formatting | bytes 2560 | tf_op jit(solution)/shard_map/reshape | solution.py:663
  3.7 1.3 %reshape.25.temporal_bias = f32[1,1280]{1,0:T(1,128)} reshape(f32[1280]{0:T(1024)} %param.18) | data formatting | bytes 10240 | tf_op jit(solution)/shard_map/reshape | solution.py:665
  5.0 1.3 %reshape.26.token_gain = f32[1,1280]{1,0:T(1,128)} reshape(f32[1280]{0:T(1024)} %param.19) | data formatting | bytes 10240 | tf_op jit(solution)/shard_map/reshape | solution.py:666
  6.3 12.9 %copy.13.spatial_hbm = bf16[3,3,1280,320]{3,2,1,0:T(8,128)(2,1)} copy(bf16[3,3,1280,320]{2,3,1,0:T(8,128)(2,1)} %param.13) | data formatting | bytes 14745600 | tf_op args[1]
  19.2 56.5 %shard_map.118 = bf16[64,1280]{1,0:T(8,128)(2,1)} custom-call(bf16[64,1280]{1,0:T(8,128)(2,1)} %bitcast.5, bf16[3,3,1280,320]{3,2,1,0:T(8,128)(2,1)} %copy.13.spatial_hbm, f32[1,320]{1,0:T(1,128)} %reshape.22.spatial_bias, f32[1,320]{1,0:T(1,128)} %reshape.23.norm_gain, f32[1,320]{1,0:T(1,128)} %reshape.24.norm_shift, bf16[3,320,1280]{2,1,0:T(8,128)(2,1)} %temporal_hbm.1, ...), custom_call_target="tpu_custom_call" | custom-call | tf_op jit(solution)/shard_map/pallas_call | solution.py:609
  75.7 1.6 %copy.16 = bf16[4,1,16,1280]{3,2,1,0:T(8,128)(2,1)} copy(bf16[4,1,16,1280]{3,2,1,0:T(8,128)(2,1)} %bitcast.4) | data formatting | bytes 327680

commit v3 on v2

--- a/solution.py
+++ b/solution.py
@@ -183,7 +183,7 @@
 ANY_SPEC = pl.BlockSpec(memory_space=pl.ANY)
 BF16 = jnp.bfloat16
 F32 = jnp.float32
-VMEM_LIMIT = 56 << 20
+VMEM_LIMIT = 54 << 20
 PARTS = 2
 
 
@@ -239,13 +239,16 @@
             copy.start()
         self.near.start()
 
+    def near_ready(self):
+        self.near.wait_recv()
+
     def finish(self):
         for copy, onward in zip(self.far, self.onward):
             copy.wait_recv()
             onward.start()
         for copy in self.far:
             copy.wait_send()
-        self.near.wait()
+        self.near.wait_send()
         for onward in self.onward:
             onward.wait()
 
@@ -277,6 +280,10 @@
     for copy in (first, second, across):
         copy.wait_send()
     return total
+
+
+def row(ref):
+    return ref[...].reshape(1, -1)
 
 
 def convolve(plane, shifted, weight, width):
@@ -300,7 +307,12 @@
     for row_off in range(3):
         for col_off in range(3):
             window = shifted[col_off, row_off * width : row_off * width + tokens, :]
-            part = jnp.dot(window, weight[row_off, col_off], preferred_element_type=F32)
+            part = lax.dot_general(
+                window,
+                weight[row_off, col_off],
+                (((1,), (1,)), ((), ())),
+                preferred_element_type=F32,
+            )
             total = part if total is None else total + part
     return total
 
@@ -405,10 +417,11 @@
     gather = Gather(latents, plane, lat_send, lat_recv)
     gather.start()
     plane[me] = latents[...]
+    gather.near_ready()
     gather.finish()
     loads[1].wait()
-    spatial = convolve(plane, shifted, spatial_w, width_cells) + spatial_bias[...]
-    act[...] = group_norm_silu(spatial, norm_gain[...], norm_shift[...], groups)
+    spatial = convolve(plane, shifted, spatial_w, width_cells) + row(spatial_bias)
+    act[...] = group_norm_silu(spatial, row(norm_gain), row(norm_shift), groups)
 
     has_prev, has_next = frame > 0, frame < frames - 1
     prev = jnp.maximum(frame - 1, 0)
@@ -483,47 +496,54 @@
         for copy in down:
             copy.wait_send()
 
-    hidden = (latents[...].astype(F32) + temporal + temporal_bias[...]).astype(BF16)
+    hidden = (latents[...].astype(F32) + temporal + row(temporal_bias)).astype(BF16)
     flat = hidden.astype(F32)
     centred = flat - jnp.mean(flat, axis=-1, keepdims=True)
     var = jnp.mean(centred * centred, axis=-1, keepdims=True)
-    normed[...] = (centred / jnp.sqrt(var + 1e-05) * token_gain[...]).astype(BF16)
+    normed[...] = (centred / jnp.sqrt(var + 1e-05) * row(token_gain)).astype(BF16)
     gather = Gather(normed, normed_all, gat_send, gat_recv)
     gather.start()
     normed_all[me] = normed[...]
-    gather.finish()
 
     tokens = act.shape[0]
-    width = got.shape[2]
-    tokens_in = normed_all[...].reshape(tokens, -1)
-    moves = []
+    width, half = got.shape[3], got.shape[4]
+    here = me // 2
+    moves = [[], [], []]
+
+    def project(pair):
+        slab = normed_all[pl.ds(2 * pair, 2)].reshape(half, -1)
+        for kind in range(3):
+            cols = jnp.dot(slab, project_w[kind], preferred_element_type=F32)
+            cols = cols.T.astype(BF16)
+            for owner in range(frames):
+                outgoing[kind, pair, owner] = cols[owner * width : (owner + 1) * width, :]
+            for turn in range(1, frames):
+                peer = lax.rem(frame + turn, frames)
+                copy = remote(
+                    outgoing.at[kind, pair, peer],
+                    got.at[kind, pair, frame],
+                    in_send.at[kind, pair, turn],
+                    in_recv.at[kind, pair, turn],
+                    "frames",
+                    peer,
+                )
+                copy.start()
+                moves[kind].append(copy)
+            got[kind, pair, frame] = outgoing[kind, pair, frame]
+
     for kind in range(3):
         loads[3 + kind].wait()
-        cols = jnp.dot(tokens_in, project_w[kind], preferred_element_type=F32)
-        cols = cols.T.astype(BF16)
-        for owner in range(frames):
-            outgoing[kind, owner] = cols[owner * width : (owner + 1) * width, :]
-        batch = []
-        for turn in range(1, frames):
-            peer = lax.rem(frame + turn, frames)
-            copy = remote(
-                outgoing.at[kind, peer],
-                got.at[kind, frame],
-                in_send.at[kind, turn],
-                in_recv.at[kind, turn],
-                "frames",
-                peer,
-            )
-            copy.start()
-            batch.append(copy)
-        got[kind, frame] = outgoing[kind, frame]
-        moves.append(batch)
+    gather.near_ready()
+    project(here)
+    gather.finish()
+    project(1 - here)
 
     for copy in moves[0]:
         copy.wait_recv()
     for source in range(frames):
-        span = slice(source * tokens, (source + 1) * tokens)
-        keys[span, :] = got[0, source].astype(F32).T.astype(BF16)
+        for pair in range(2):
+            begin = source * tokens + pair * half
+            keys[begin : begin + half, :] = got[0, pair, source].astype(F32).T.astype(BF16)
     for copy in moves[1]:
         copy.wait_recv()
     scale = 1.0 / math.sqrt(HD)
@@ -533,7 +553,9 @@
         peer = lax.rem(frame + turn, frames)
         for head in range(heads):
             cols = slice(head * HD, (head + 1) * HD)
-            query = got[1, peer, cols, :]
+            query = jnp.concatenate(
+                [got[1, 0, peer, cols, :], got[1, 1, peer, cols, :]], axis=1
+            )
             scores = jnp.dot(keys[:, cols], query, preferred_element_type=F32) * scale
             weights = jnp.exp(scores - jnp.max(scores, axis=0, keepdims=True))
             sums.append(jnp.sum(weights, axis=0, keepdims=True))
@@ -541,43 +563,62 @@
     for copy in moves[2]:
         copy.wait_recv()
     for source in range(frames):
-        values[:, source * tokens : (source + 1) * tokens] = got[2, source]
-    returns = []
+        for pair in range(2):
+            begin = source * tokens + pair * half
+            values[:, begin : begin + half] = got[2, pair, source]
+    returns = [[], []]
+
+    def give_back(step, pair, turn):
+        peer = lax.rem(frame + turn, frames)
+        copy = remote(
+            done.at[pair, peer],
+            back.at[pair, frame],
+            out_send.at[pair, turn],
+            out_recv.at[pair, turn],
+            "frames",
+            peer,
+        )
+        copy.start()
+        returns[step].append(copy)
+
     for turn in range(1, frames + 1):
         peer = lax.rem(frame + turn, frames)
         for head in range(heads):
             cols = slice(head * HD, (head + 1) * HD)
             place = (turn - 1) * heads + head
             numerator = jnp.dot(values[cols, :], probs[place], preferred_element_type=F32)
-            done[peer, cols, :] = (numerator / sums[place]).astype(BF16)
+            result = (numerator / sums[place]).astype(BF16)
+            for pair in range(2):
+                done[pair, peer, cols, :] = result[:, pair * half : (pair + 1) * half]
         if turn < frames:
-            copy = remote(
-                done.at[peer],
-                back.at[frame],
-                out_send.at[turn],
-                out_recv.at[turn],
-                "frames",
-                peer,
+            give_back(0, 1 - here, turn)
+    for turn in range(1, frames):
+        give_back(1, here, turn)
+    for pair in range(2):
+        back[pair, frame] = done[pair, frame]
+    loads[6].wait()
+
+    def collect(step, pair):
+        for copy in returns[step]:
+            copy.wait_recv()
+        rows = pl.ds(pl.multiple_of(pair * half, half), half)
+        for source in range(frames):
+            att[rows, source * width : (source + 1) * width] = (
+                back[pair, source].astype(F32).T.astype(BF16)
             )
-            copy.start()
-            returns.append(copy)
-    back[frame] = done[frame]
-    loads[6].wait()
-    for copy in returns:
-        copy.wait_recv()
-    for source in range(frames):
-        att[:, source * width : (source + 1) * width] = (
-            back[source].astype(F32).T.astype(BF16)
-        )
 
     def mixed_term(block, turn):
+        if turn == 0:
+            collect(0, 1 - here)
+        if turn == 2:
+            collect(1, here)
         return jnp.dot(att[rows_of(block), :], output_w[...], preferred_element_type=F32)
 
     mixed = reduce_rows(
         mixed_term, sent.at[1], got_near.at[1], got_far.at[1], sum_send.at[1], sum_recv.at[1]
     )
     out_ref[...] = (hidden.astype(F32) + mixed).astype(BF16)
-    for batch in moves + [returns]:
+    for batch in moves + returns:
         for copy in batch:
             copy.wait_send()
 
@@ -617,7 +658,7 @@
         out_specs=VMEM_SPEC,
         scratch_shapes=[
             pltpu.VMEM(block.shape, BF16),
-            pltpu.VMEM(spatial_weight.shape, BF16),
+            pltpu.VMEM(spatial_weight.shape[:2] + (local_out, channels), BF16),
             pltpu.VMEM(temporal_weight.shape, BF16),
             pltpu.VMEM((3,) + query_weight.shape, BF16),
             pltpu.VMEM(output_weight.shape, BF16),
@@ -627,13 +668,13 @@
             pltpu.VMEM((2, tokens, local_out), BF16),
             pltpu.VMEM(block.shape, BF16),
             pltpu.VMEM((peers,) + block.shape, BF16),
-            pltpu.VMEM((3, frames, width, tokens), BF16),
-            pltpu.VMEM((3, frames, width, tokens), BF16),
+            pltpu.VMEM((3, 2, frames, width, tokens // 2), BF16),
+            pltpu.VMEM((3, 2, frames, width, tokens // 2), BF16),
             pltpu.VMEM((frames * tokens, width), BF16),
             pltpu.VMEM((width, frames * tokens), BF16),
             pltpu.VMEM((frames * heads, frames * tokens, tokens), BF16),
-            pltpu.VMEM((frames, width, tokens), BF16),
-            pltpu.VMEM((frames, width, tokens), BF16),
+            pltpu.VMEM((2, frames, width, tokens // 2), BF16),
+            pltpu.VMEM((2, frames, width, tokens // 2), BF16),
             pltpu.VMEM((tokens, frames * width), BF16),
             pltpu.VMEM((2, 3) + block.shape, BF16),
             pltpu.VMEM((2, 2) + block.shape, BF16),
@@ -645,10 +686,10 @@
             DMA((2, peers)),
             DMA((links,)),
             DMA((links,)),
-            DMA((3, frames)),
-            DMA((3, frames)),
-            DMA((frames,)),
-            DMA((frames,)),
+            DMA((3, 2, frames)),
+            DMA((3, 2, frames)),
+            DMA((2, frames)),
+            DMA((2, frames)),
             DMA((2, 3)),
             DMA((2, 3)),
         ],
@@ -657,13 +698,13 @@
         ),
     )(
         block,
-        spatial_weight,
-        spatial_bias.reshape(1, -1),
-        norm_gain.reshape(1, -1),
-        norm_shift.reshape(1, -1),
+        jnp.swapaxes(spatial_weight, 2, 3),
+        spatial_bias,
+        norm_gain,
+        norm_shift,
         temporal_weight,
-        temporal_bias.reshape(1, -1),
-        token_gain.reshape(1, -1),
+        temporal_bias,
+        token_gain,
         query_weight,
         key_weight,
         value_weight,
@@ -682,7 +723,7 @@
             peers == 4
             and latents.shape[1] == 1
             and heads % frames == 0
-            and tokens % 128 == 0
+            and tokens % 256 == 0
             and latents.shape[2] % 16 == 0
             and latents.shape[0] * latents.shape[2] % (16 * PARTS) == 0
         )

time: 77.9 us -> 54.6 us (0.70)
  local copies, waits for them, and re-layouts: 20.8 us -> 1.59 us
  Pallas kernels: 56.5 us -> 52.8 us
    unnamed x2 -> x1, local copies, waits for them, and re-layouts: 14.5 us -> 1.59 us
    reshape x5 -> x0, local copies, waits for them, and re-layouts: 6.33 us -> none  [the longest x1 1.3 us: body_fast(): token_gain.reshape(1, -1)]
    pallas_call x1, Pallas kernels: 56.5 us -> 52.8 us  [body_fast(): pl.pallas_call(functools.partial(block_kernel, frames, width_cells, NORM_...]
where the time goes in v3:
time: 54.6 us; the launch traced here: 54.4 us
  Pallas kernels  52.8 us (97%)
  local copies, waits for them, and re-layouts  1.59 us (3%)
    pallas_call x1, Pallas kernels, body_fast(): pl.pallas_call(functools.partial(block_kernel, frames, width_cells, NORM_...  52.8 us
    unnamed x1, local copies, waits for them, and re-layouts  1.59 us

profile of v3, /device:TPU:0, one launch (start us, length us, event | category | flops | bytes accessed | tf_op | source)
XLA Modules:
  0.0 54.4 jit_solution(13651529720119221767)
XLA Ops:
  0.0 52.8 %shard_map.118 = bf16[64,1280]{1,0:T(8,128)(2,1)} custom-call(bf16[64,1280]{1,0:T(8,128)(2,1)} %bitcast.7, bf16[3,3,320,1280]{3,2,1,0:T(8,128)(2,1)} %bitcast.5, f32[320]{0:T(512)} %spatial_bias.1, f32[320]{0:T(512)} %norm_gain.1, f32[320]{0:T(512)} %norm_shift.1, bf16[3,320,1280]{2,1,0:T(8,128)(2,1)} %temporal_hbm.1, f32[1280]{0:T(1024)} %temporal_bias.1, ...), custom_call_target="tpu_custom_call" | custom-call | tf_op jit(solution)/shard_map/pallas_call | solution.py:650
  52.8 1.6 %copy.15 = bf16[4,1,16,1280]{3,2,1,0:T(8,128)(2,1)} copy(bf16[4,1,16,1280]{3,2,1,0:T(8,128)(2,1)} %bitcast.6) | data formatting | bytes 327680

commit v4 on v3

--- a/solution.py
+++ b/solution.py
@@ -286,32 +286,42 @@
     return ref[...].reshape(1, -1)
 
 
-def convolve(plane, shifted, weight, width):
-    blocks, size, channels = plane.shape
-    tokens = blocks * size
-    edge = jnp.zeros((width, channels), BF16)
-    column = lax.broadcasted_iota(jnp.int32, (size, channels), 0) % width
+def clear_edges(shifted, width, row_after):
+    edge = jnp.zeros((width, shifted.shape[2]), BF16)
+    tall = shifted.shape[1]
     for offset in range(3):
         shifted[offset, :width, :] = edge
-        shifted[offset, tokens + width :, :] = edge
-    for block in range(blocks):
-        rows = slice(width + block * size, width + (block + 1) * size)
-        value = plane[block]
-        wide = value.astype(F32)
-        before = jnp.where(column == 0, 0.0, pltpu.roll(wide, 1, 0))
-        after = jnp.where(column == width - 1, 0.0, pltpu.roll(wide, size - 1, 0))
-        shifted[0, rows, :] = before.astype(BF16)
-        shifted[1, rows, :] = value
-        shifted[2, rows, :] = after.astype(BF16)
+        shifted[offset, tall - width :, :] = edge
+        shifted[offset, pl.ds(pl.multiple_of(row_after, width), width), :] = edge
+
+
+def shift_block(value, shifted, block, width):
+    size = value.shape[0]
+    column = lax.broadcasted_iota(jnp.int32, value.shape, 0) % width
+    rows = pl.ds(pl.multiple_of(width + block * size, width), size)
+    wide = value.astype(F32)
+    before = jnp.where(column == 0, 0.0, pltpu.roll(wide, 1, 0))
+    after = jnp.where(column == width - 1, 0.0, pltpu.roll(wide, size - 1, 0))
+    shifted[0, rows, :] = before.astype(BF16)
+    shifted[1, rows, :] = value
+    shifted[2, rows, :] = after.astype(BF16)
+
+
+def tap(shifted, weight, begin, count, width, row_off, col_off):
+    return lax.dot_general(
+        shifted[col_off, pl.ds(pl.multiple_of(begin, width), count), :],
+        weight[row_off, col_off],
+        (((1,), (1,)), ((), ())),
+        preferred_element_type=F32,
+    )
+
+
+def convolve(shifted, weight, begin, count, width):
     total = None
     for row_off in range(3):
         for col_off in range(3):
-            window = shifted[col_off, row_off * width : row_off * width + tokens, :]
-            part = lax.dot_general(
-                window,
-                weight[row_off, col_off],
-                (((1,), (1,)), ((), ())),
-                preferred_element_type=F32,
+            part = tap(
+                shifted, weight, begin + row_off * width, count, width, row_off, col_off
             )
             total = part if total is None else total + part
     return total
@@ -359,6 +369,7 @@
     output_w,
     plane,
     shifted,
+    conv,
     act,
     halo,
     normed,
@@ -416,17 +427,45 @@
     loads[0].wait()
     gather = Gather(latents, plane, lat_send, lat_recv)
     gather.start()
-    plane[me] = latents[...]
+    size = latents.shape[0]
+    slab = 2 * size
+    chip = me // 2
+    mine, other = chip * slab, (1 - chip) * slab
+    border = slab - width_cells + chip * width_cells
+    beyond = slab - chip * width_cells
+    clear_edges(shifted, width_cells, beyond + width_cells)
+    shift_block(latents[...], shifted, me, width_cells)
     gather.near_ready()
+    shift_block(plane[near], shifted, near, width_cells)
+    loads[1].wait()
+    conv[pl.ds(pl.multiple_of(mine, slab), slab), :] = convolve(
+        shifted, spatial_w, mine, slab, width_cells
+    )
     gather.finish()
-    loads[1].wait()
-    spatial = convolve(plane, shifted, spatial_w, width_cells) + row(spatial_bias)
+    shift_block(plane[far], shifted, far, width_cells)
+    shift_block(plane[far ^ 1], shifted, far ^ 1, width_cells)
+    conv[pl.ds(pl.multiple_of(other, slab), slab), :] = convolve(
+        shifted, spatial_w, other, slab, width_cells
+    )
+    line = pl.ds(pl.multiple_of(border, width_cells), width_cells)
+    late = conv[line, :]
+    for col_off in range(3):
+        late += tap(
+            shifted,
+            spatial_w,
+            beyond + width_cells,
+            width_cells,
+            width_cells,
+            2 - 2 * chip,
+            col_off,
+        )
+    conv[line, :] = late
+    spatial = conv[...] + row(spatial_bias)
     act[...] = group_norm_silu(spatial, row(norm_gain), row(norm_shift), groups)
 
     has_prev, has_next = frame > 0, frame < frames - 1
     prev = jnp.maximum(frame - 1, 0)
     later = jnp.minimum(frame + 1, frames - 1)
-    size = latents.shape[0]
 
     def rows_of(block):
         return pl.ds(pl.multiple_of(block * size, size), size)
@@ -664,6 +703,7 @@
             pltpu.VMEM(output_weight.shape, BF16),
             pltpu.VMEM((peers,) + block.shape, BF16),
             pltpu.VMEM((3, tokens + 2 * width_cells, channels), BF16),
+            pltpu.VMEM((tokens, local_out), F32),
             pltpu.VMEM((tokens, local_out), BF16),
             pltpu.VMEM((2, tokens, local_out), BF16),
             pltpu.VMEM(block.shape, BF16),

time: 54.6 us -> 57.2 us (1.048)
  Pallas kernels: 52.8 us -> 55.4 us
    pallas_call x1, Pallas kernels: 52.8 us -> 55.4 us  [body_fast(): pl.pallas_call(functools.partial(block_kernel, frames, width_cells, NORM_...]
where the time goes in v4:
time: 57.2 us; the launch traced here: 57 us
  Pallas kernels  55.4 us (97%)
  local copies, waits for them, and re-layouts  1.59 us (3%)
    pallas_call x1, Pallas kernels, body_fast(): pl.pallas_call(functools.partial(block_kernel, frames, width_cells, NORM_...  55.4 us
    unnamed x1, local copies, waits for them, and re-layouts  1.59 us

profile of v4, /device:TPU:0, one launch (start us, length us, event | category | flops | bytes accessed | tf_op | source)
XLA Modules:
  0.0 57.0 jit_solution(8029779880670162536)
XLA Ops:
  0.0 55.4 %shard_map.118 = bf16[64,1280]{1,0:T(8,128)(2,1)} custom-call(bf16[64,1280]{1,0:T(8,128)(2,1)} %bitcast.7, bf16[3,3,320,1280]{3,2,1,0:T(8,128)(2,1)} %bitcast.5, f32[320]{0:T(512)} %spatial_bias.1, f32[320]{0:T(512)} %norm_gain.1, f32[320]{0:T(512)} %norm_shift.1, bf16[3,320,1280]{2,1,0:T(8,128)(2,1)} %temporal_hbm.1, f32[1280]{0:T(1024)} %temporal_bias.1, ...), custom_call_target="tpu_custom_call" | custom-call | tf_op jit(solution)/shard_map/pallas_call | solution.py:689
  55.4 1.6 %copy.15 = bf16[4,1,16,1280]{3,2,1,0:T(8,128)(2,1)} copy(bf16[4,1,16,1280]{3,2,1,0:T(8,128)(2,1)} %bitcast.6) | data formatting | bytes 327680
